TPU v7x, 32 devices: a whole 2x2x4 slice. The times are simulated.
32 devices in a mesh: blk: 8 (over y, x, core), wide: 4 (over z).
Axes of the slice: x: 2, y: 2, z: 4, core: 2. Of those that a mesh axis runs over, the one named last changes fastest.
Arguments:
- coupling: bfloat16 [1024, 8, 2, 512], P('blk', 'wide'), may hold values from -0.09375 to 0.09375
- rp_cells: int32 [3, 1024], replicated, may hold values from -8 to 7
- re_cells: int32 [3, 8], P(None, 'wide'), may hold values from -8 to 7
- q_points: int32 [3, 2048], P(None, 'blk'), may hold values from 0 to 31
- k_points: int32 [3, 2], replicated, may hold values from 0 to 31
- mode_energy: float32 [16, 2048], P(None, 'blk'), may hold values from 0.02 to 1
Outputs:
- bloch_coupling: float32 [2, 2, 512, 2048], P(None, None, 'wide', 'blk')
All inputs are finite; a program needn't handle non-finite values.
Results may differ from a plain program's by a relative error of at most 0.002.
Values may be sent and summed in bfloat16 or wider, within the bound.
No kernel may reach another device: no remote copies, remote signals or barrier semaphores. Data moves between devices by JAX's collectives and lax.ppermute only.
A program may use at most 64 MiB of HBM per device.

v0:
```python
import math

import jax
import jax.numpy as jnp
from jax import lax
from jax.sharding import PartitionSpec as P

MODES = 16
MESHQ = 32
MESHK = 32


def phase_parts(left, right, modulus):
    whole = jnp.sum(left[:, :, None] * right[:, None, :], axis=0)
    angle = jnp.mod(whole, modulus).astype(jnp.float32) * (2.0 * math.pi / modulus)
    return (jnp.cos(angle), jnp.sin(angle))


def q_table(q_points, vectors):
    cosine, sine = phase_parts(q_points, vectors, MESHQ)
    return jnp.concatenate([cosine, sine], axis=0).astype(jnp.bfloat16)


def entry_weights(mode_energy, offset, entries):
    weight = 1.0 / jnp.sqrt(2.0 * mode_energy)
    entry_index = offset + jnp.arange(entries, dtype=jnp.int32)
    selector = (
        (entry_index % MODES)[:, None] == jnp.arange(MODES, dtype=jnp.int32)[None, :]
    ).astype(jnp.float32)
    return jnp.dot(selector, weight, precision=lax.Precision.HIGHEST)


def on_device(coupling, rp_cells, re_cells, q_points, k_points, mode_energy):
    slab_rows = coupling.shape[0]
    q_local = q_points.shape[1]
    high = lax.Precision.HIGHEST
    moved = lax.all_to_all(coupling, "wide", split_axis=3, concat_axis=1, tiled=True)
    cells = lax.all_gather(re_cells, "wide", axis=1, tiled=True)
    entries = moved.shape[3]
    offset = lax.axis_index("wide") * entries
    cell_count = moved.shape[1]
    flat = moved.reshape(slab_rows, cell_count * 2 * entries)
    table = q_table(q_points, rp_cells)
    summed = lax.dot_general(
        lax.all_gather(flat, "blk", axis=0, tiled=True),
        table,
        (((0,), (1,)), ((), ())),
        preferred_element_type=jnp.float32,
    )
    summed = summed.reshape(cell_count, 2, entries, 2, q_local)
    real = summed[:, 0, :, 0] - summed[:, 1, :, 1]
    imag = summed[:, 1, :, 0] + summed[:, 0, :, 1]
    entry_weight = entry_weights(mode_energy, offset, entries)
    real = real * entry_weight[None]
    imag = imag * entry_weight[None]
    k_cos, k_sin = phase_parts(k_points, cells, MESHK)
    part_re = jnp.einsum("kr,req->keq", k_cos, real, precision=high) - jnp.einsum(
        "kr,req->keq", k_sin, imag, precision=high
    )
    part_im = jnp.einsum("kr,req->keq", k_cos, imag, precision=high) + jnp.einsum(
        "kr,req->keq", k_sin, real, precision=high
    )
    partial_value = jnp.stack([part_re, part_im], axis=1)
    return partial_value


def solution(mesh):
    in_specs = (
        P("blk", "wide", None, None),
        P(),
        P(None, "wide"),
        P(None, "blk"),
        P(),
        P(None, "blk"),
    )
    out_specs = P(None, None, "wide", "blk")
    return jax.shard_map(
        on_device, mesh=mesh, in_specs=in_specs, out_specs=out_specs, check_vma=False
    )
```

profile of v0, /device:TPU:0, one launch (start us, length us, event | category | flops | bytes accessed | tf_op | source)
XLA Modules:
  0.0 106.6 jit_solution(10636870011201941082)
XLA Ops:
  6.5 0.0 all-gather.3.cloned.1.call-start
  6.6 2.4 %copy.42 = bf16[128,2,2,512]{0,2,1,3:T(2,128)(2,1)S(1)} copy(bf16[128,2,2,512]{3,2,1,0:T(2,128)(2,1)} %param.6) | data formatting | bytes 1048576 | tf_op args[0]
  9.0 20.6 %all_to_all.15 = bf16[128,2,2,512]{0,2,1,3:T(2,128)(2,1)S(1)} all-to-all(bf16[128,2,2,512]{0,2,1,3:T(2,128)(2,1)S(1)} %copy.42), channel_id=1, replica_groups=mesh['blk'=8,'wide'=4] {'wide'}, dimensions={3} | all-to-all | bytes 1048576 | tf_op jit(solution)/shard_map/all_to_all | solution.py:37
  29.6 0.1 copy.43
  29.7 0.8 copy.44
  30.5 0.0 all-gather.3.cloned.1.call-update
  30.5 0.0 copy-done.4
  30.5 9.0 %all-gather = s32[4,2,3]{2,1,0:T(2,128)S(1)} all-gather(s32[1,2,3]{2,1,0:T(2,128)S(1)} %bitcast.40), channel_id=1, replica_groups=mesh['blk'=8,'wide'=4] {'wide'}, dimensions={0}, use_global_device_ids=true | all-gather | bytes 120 | tf_op jit(solution)/shard_map/all_gather | solution.py:38
  39.6 0.1 copy.41
  39.7 0.0 copy-done.5
  39.7 0.1 copy.40
  39.8 0.1 multiply_reduce_fusion.1
  39.8 0.1 fusion.25
  40.0 0.0 copy-done.1
  40.0 0.0 copy-done.3
  40.0 0.3 multiply_reduce_fusion
  40.3 0.3 fusion.10
  40.5 4.2 %cosine_convert_fusion = (bf16[256,1024]{1,0:T(8,128)(2,1)S(1)}, bf16[256,1024]{1,0:T(8,128)(2,1)S(1)}) fusion(s32[256,1024]{1,0:T(8,128)S(1)} %multiply_reduce_fusion), kind=kLoop, calls=%fused_computation.18 | loop fusion | flops 3932160 | bytes 2097152 | tf_op jit(solution)/shard_map/convert
  44.8 22.4 %all-gather.3.cloned.1.call-done = bf16[1024,2048]{0,1:T(8,128)(2,1)} async-done(((bf16[128,2048]{0,1:T(8,128)(2,1)}), bf16[1024,2048]{0,1:T(8,128)(2,1)}) %all-gather.3.cloned.1.call-update) | async-done | bytes 4194320 | tf_op jit(solution)/shard_map/all_gather | solution.py:45
  67.1 6.5 %convolution_bitcast_fusion = f32[2048,512]{0,1:T(8,128)} fusion(bf16[1024,2048]{0,1:T(8,128)(2,1)} %all-gather.3.cloned.1.call-done, bf16[256,1024]{1,0:T(8,128)(2,1)S(1)} %get-tuple-element.12, bf16[256,1024]{1,0:T(8,128)(2,1)S(1)} %get-tuple-element.11), kind=kOutput, calls=%fused_computation | convolution fusion | flops 2149580800 | bytes 9437184 | tf_op jit(solution)/shard_map/dot_general | solution.py:44
  73.7 6.6 %reshape.30 = f32[8,2,128,2,256]{2,1,0,4,3:T(2,128)} reshape(f32[2048,512]{0,1:T(8,128)} %convolution_bitcast_fusion) | data formatting | bytes 8388608 | tf_op jit(solution)/shard_map/reshape | solution.py:50
  80.3 8.1 %fusion.27 = (f32[8,1,128,1,256]{2,1,0,4,3:T(1,128)S(1)}, f32[8,1,128,1,256]{2,1,0,4,3:T(1,128)}, f32[8,1,128,1,256]{2,1,0,4,3:T(1,128)S(1)}, f32[8,1,128,1,256]{2,1,0,4,3:T(1,128)}) fusion(f32[8,2,128,2,256]{2,1,0,4,3:T(2,128)} %reshape.30), kind=kLoop, calls=%fused_computation.46 | loop fusion | bytes 8388608 | tf_op jit(solution)/shard_map/slice | solution.py:51
  88.4 0.6 copy.50
  89.0 0.6 copy.51
  89.6 1.6 %copy.52 = f32[8,1,128,1,256]{4,0,2,3,1:T(8,128)S(1)} copy(f32[8,1,128,1,256]{2,1,0,4,3:T(1,128)} %get-tuple-element.8) | data formatting | bytes 2097152
  91.2 2.3 %copy.53 = f32[8,1,128,1,256]{4,0,2,3,1:T(8,128)} copy(f32[8,1,128,1,256]{2,1,0,4,3:T(1,128)} %get-tuple-element.10) | data formatting | bytes 2097152
  93.5 1.0 fusion.8
  94.5 2.2 %fusion.9 = f32[2,128,256]{2,0,1:T(2,128)S(1)} fusion(f32[8,1,128,1,256]{4,0,2,3,1:T(8,128)S(1)} %copy.52, f32[8,1,128,1,256]{4,0,2,3,1:T(8,128)} %copy.53, f32[128,256]{1,0:T(8,128)S(1)} %fusion.10, f32[2,8]{1,0:T(2,128)S(1)} %cos.6), kind=kOutput, calls=%fused_computation.21 | convolution fusion | flops 6815744 | bytes 2490432 | tf_op jit(solution)/shard_map/kr,req->keq/dot_general | solution.py:60
  96.7 1.0 fusion.1
  97.7 1.0 fusion
  98.7 0.2 pad_maximum_fusion
  98.9 0.8 copy.49
  (10 shorter events, 0.1 us)
Async XLA Ops:
  6.5 24.0 %copy-start.4 = (s32[3,2]{0,1:T(2,128)S(1)}, s32[3,2]{0,1:T(2,128)}, u32[]{:S(2)}) copy-start(s32[3,2]{0,1:T(2,128)} %param.8) | copy-start | bytes 76
  6.5 33.1 %copy-start.5 = (s32[3,2]{0,1:T(2,128)S(1)}, s32[3,2]{0,1:T(2,128)}, u32[]{:S(2)}) copy-start(s32[3,2]{0,1:T(2,128)} %param.10) | copy-start | bytes 76
  6.5 33.4 %copy-start.1 = (s32[3,1024]{1,0:T(4,128)S(1)}, s32[3,1024]{1,0:T(4,128)}, u32[]{:S(2)}) copy-start(s32[3,1024]{1,0:T(4,128)} %param.7) | copy-start | bytes 36868
  6.5 33.4 %copy-start.3 = (s32[3,256]{1,0:T(4,128)S(1)}, s32[3,256]{1,0:T(4,128)}, u32[]{:S(2)}) copy-start(s32[3,256]{1,0:T(4,128)} %param.9) | copy-start | bytes 9220
  6.5 33.7 %copy-start.2 = (f32[16,256]{1,0:T(8,128)S(1)}, f32[16,256]{1,0:T(8,128)}, u32[]{:S(2)}) copy-start(f32[16,256]{1,0:T(8,128)} %param.11) | copy-start | bytes 49156
  6.5 60.6 %all-gather.3.cloned.1.call-start = ((), (), s32[]{:S(2)}) async-start(), calls=%async_computation.1 | async-start | bytes 4718592 | tf_op jit(solution)/shard_map/all_gather | solution.py:45
  93.5 3.2 %copy-start = (f32[8,1,128,1,256]{4,0,2,3,1:T(8,128)S(1)}, f32[8,1,128,1,256]{4,0,2,3,1:T(8,128)}, u32[]{:S(2)}) copy-start(f32[8,1,128,1,256]{4,0,2,3,1:T(8,128)} %copy.53) | copy-start | bytes 3145732
Sparse Core Ops, SparseCore 0:
  30.6 36.4 all-gather.2
where the time goes:
time: 107 us
  blocking collectives  29.7 us (28%)
  local copies, waits for them, and re-layouts  24.1 us (23%)
  waiting for transfers between devices  22.4 us (21%)
  between operations  13.6 us (13%)
  matrix products  12 us (11%)
  other arithmetic  4.91 us (5%)
    all_gather x1, waiting for transfers between devices, on_device(): lax.all_gather(flat, 'blk', axis=0, tiled=True)  22.4 us
    all_to_all x1, blocking collectives, on_device(): lax.all_to_all(coupling, 'wide', split_axis=3, concat_axis=1, tiled=True)  20.6 us
    all_gather x1, blocking collectives, on_device(): cells = lax.all_gather(re_cells, 'wide', axis=1, tiled=True)  9.04 us
    slice x1, local copies, waits for them, and re-layouts, on_device(): real = summed[:, 0, :, 0] - summed[:, 1, :, 1]  8.14 us
    unnamed x19, local copies, waits for them, and re-layouts  7.58 us
    reshape x1, local copies, waits for them, and re-layouts, on_device(): summed = summed.reshape(cell_count, 2, entries, 2, q_local)  6.59 us
    dot_general x1, matrix products, on_device(): lax.dot_general(lax.all_gather(flat, 'blk', axis=0, tiled=True), table, (...  6.53 us
    another operation x1, other arithmetic  4.24 us
  transfers between devices with their start and end apart: 1, of which 1 were waited for; matrix products, arithmetic and copies ran while one was open for 5% of the time, Pallas kernels for 0%

commit v1 on v0

v1 whole, which is shorter than its diff:
```python
import functools
import math

import jax
import jax.numpy as jnp
from jax import lax
from jax.experimental import pallas as pl
from jax.experimental.pallas import tpu as pltpu
from jax.sharding import PartitionSpec as P

MODES = 16
MESHQ = 32
MESHK = 32
LANES = 128
TAIL = 4
SHARES = (1,)


def xor_pairs(count, step):
    return [(i, i ^ step) for i in range(count)]


def swap(value, axis, count, step):
    return lax.ppermute(value, axis, xor_pairs(count, step))


def slice_kernel(starts, steps, entries, x_ref, tail_ref, *rest):
    outs, sem = rest[:-1], rest[-1]
    me = lax.axis_index("wide")
    copies = []
    for c, (first, rows) in enumerate(starts):
        for j, step in enumerate(steps):
            out = outs[c * len(steps) + j]
            column = pl.multiple_of((me ^ step) * entries, LANES)
            copies.append(
                pltpu.make_async_copy(
                    x_ref.at[pl.ds(first, rows), :, :, pl.ds(column, entries)],
                    out.at[pl.ds(0, rows)],
                    sem.at[2 * len(copies)],
                )
            )
    tails = []
    for i, out in enumerate(outs):
        rows = starts[i // len(steps)][1]
        tails.append(
            pltpu.make_async_copy(tail_ref, out.at[pl.ds(rows, TAIL)], sem.at[2 * i + 1])
        )
    for copy in copies + tails:
        copy.start()
    for copy in copies + tails:
        copy.wait()


def cut(coupling, tail, starts, steps, entries):
    cells = coupling.shape[1]
    shapes = []
    for _, rows in starts:
        for _ in steps:
            shapes.append(
                jax.ShapeDtypeStruct((rows + TAIL, cells, 2, entries), coupling.dtype)
            )
    return pl.pallas_call(
        functools.partial(slice_kernel, starts, steps, entries),
        out_shape=shapes,
        in_specs=[pl.BlockSpec(memory_space=pl.ANY)] * 2,
        out_specs=[pl.BlockSpec(memory_space=pl.ANY)] * len(shapes),
        scratch_shapes=[pltpu.SemaphoreType.DMA((2 * len(shapes),))],
        name="cut",
    )(coupling, tail)


def combine_kernel(rows, cells, entries, waves, *refs):
    ins = refs[: -2]
    out, work = refs[-2], refs[-1]
    per = 2 * cells
    phases = []
    for i, ref in enumerate(ins):
        work[i] = ref[...].astype(jnp.float32)
    for i in range(len(ins)):
        angle = work[i, pl.ds(rows * per, 8), :] * (2.0 * math.pi / MESHK)
        phases.append((jnp.cos(angle), jnp.sin(angle)))
    step = 32
    for first in range(0, rows, step):
        re = [None] * waves
        im = [None] * waves
        for i in range(len(ins)):
            cos, sin = phases[i]
            for r in range(cells):
                a = work[i, pl.ds(first * per + 2 * r, step, stride=per), :]
                b = work[i, pl.ds(first * per + 2 * r + 1, step, stride=per), :]
                for k in range(waves):
                    at = r * waves + k
                    c = cos[at : at + 1, :]
                    s = sin[at : at + 1, :]
                    x = c * a - s * b
                    y = c * b + s * a
                    re[k] = x if re[k] is None else re[k] + x
                    im[k] = y if im[k] is None else im[k] + y
        for k in range(waves):
            lanes = pl.ds(k * entries, entries)
            out[pl.ds(first, step), lanes] = re[k].astype(out.dtype)
            out[pl.ds(rows + first, step), lanes] = im[k].astype(out.dtype)


def combine(blocks, rows, cells, entries, waves):
    flat = [b.reshape(b.shape[0] * 2 * cells, entries) for b in blocks]
    full = flat[0].shape[0]
    return pl.pallas_call(
        functools.partial(combine_kernel, rows, cells, entries, waves),
        out_shape=jax.ShapeDtypeStruct((2 * rows, waves * entries), jnp.bfloat16),
        in_specs=[pl.BlockSpec(memory_space=pltpu.VMEM)] * len(flat),
        out_specs=pl.BlockSpec(memory_space=pltpu.VMEM),
        scratch_shapes=[pltpu.VMEM((len(flat), full, entries), jnp.float32)],
        name="combine",
    )(*flat)


def table_kernel(starts, slab, rp_ref, q_ref, out_ref):
    lane = lax.broadcasted_iota(jnp.int32, (8, LANES), 1) % MESHQ
    angle = lane.astype(jnp.float32) * (2.0 * math.pi / MESHQ)
    cos_table = jnp.cos(angle)
    sin_table = jnp.sin(angle)
    blocks = out_ref.shape[0]
    q_local = q_ref.shape[1]
    step = 32

    for block in range(blocks):
        row = 0
        for first, rows in starts:
            n = lax.dot_general(
                rp_ref[:, pl.ds(block * slab, slab)],
                q_ref[...],
                (((0,), (0,)), ((), ())),
                preferred_element_type=jnp.float32,
            )
            m = n - MESHQ * jnp.floor(n * (1.0 / MESHQ))
            index = m.astype(jnp.int32)
            for top in range(first, first + rows, step):
                for left in range(0, q_local, LANES):
                    cos_rows = []
                    sin_rows = []
                    for sub in range(0, step, 8):
                        at = index[top + sub : top + sub + 8, left : left + LANES]
                        cos_rows.append(
                            jnp.take_along_axis(
                                cos_table, at, axis=1, mode="promise_in_bounds"
                            )
                        )
                        sin_rows.append(
                            jnp.take_along_axis(
                                sin_table, at, axis=1, mode="promise_in_bounds"
                            )
                        )
                    c = jnp.concatenate(cos_rows, axis=0)
                    s = jnp.concatenate(sin_rows, axis=0)
                    re_rows = pl.ds(row + top - first, step)
                    im_rows = pl.ds(row + rows + top - first, step)
                    near = pl.ds(left, LANES)
                    far = pl.ds(q_local + left, LANES)
                    cb = c.astype(jnp.bfloat16)
                    sb = s.astype(jnp.bfloat16)
                    nb = (-s).astype(jnp.bfloat16)
                    out_ref[block, re_rows, near] = cb
                    out_ref[block, re_rows, far] = sb
                    out_ref[block, im_rows, near] = nb
                    out_ref[block, im_rows, far] = cb
            row += 2 * rows


def table(rp_cells, q_points, starts, slab):
    blocks = rp_cells.shape[1] // slab
    q_local = q_points.shape[1]
    pad = ((0, 16 - rp_cells.shape[0]), (0, 0))
    rp = jnp.pad(rp_cells.astype(jnp.bfloat16), pad)
    q = jnp.pad(q_points.astype(jnp.bfloat16), pad)
    return pl.pallas_call(
        functools.partial(table_kernel, starts, slab),
        out_shape=jax.ShapeDtypeStruct((blocks, 2 * slab, 2 * q_local), jnp.bfloat16),
        in_specs=[pl.BlockSpec(memory_space=pltpu.VMEM)] * 2,
        out_specs=pl.BlockSpec(memory_space=pltpu.VMEM),
        cost_estimate=pl.CostEstimate(
            flops=8 * blocks * slab * q_local * 10,
            bytes_accessed=blocks * slab * q_local * 8,
            transcendentals=0,
        ),
        name="table",
    )(rp, q)


def product_kernel(pieces, waves, entries, table_ref, energy_ref, *refs):
    ins, out, acc = refs[: len(pieces)], refs[-2], refs[-1]
    me = lax.axis_index("blk")
    q_local = energy_ref.shape[1]
    for i, (step, row, rows) in enumerate(pieces):
        part = lax.dot_general(
            ins[i][...],
            table_ref[me ^ step, pl.ds(row, rows), :],
            (((0,), (0,)), ((), ())),
            preferred_element_type=jnp.float32,
        )
        if i == 0:
            acc[...] = part
        else:
            acc[...] += part
    weight = 1.0 / jnp.sqrt(2.0 * energy_ref[...])
    for k in range(waves):
        for part in range(2):
            for e in range(0, entries, MODES):
                out[k, part, pl.ds(e, MODES), :] = (
                    acc[pl.ds(k * entries + e, MODES), pl.ds(part * q_local, q_local)]
                    * weight
                )


def product(tables, energy, blocks, pieces, waves, entries):
    q_local = energy.shape[1]
    return pl.pallas_call(
        functools.partial(product_kernel, pieces, waves, entries),
        out_shape=jax.ShapeDtypeStruct((waves, 2, entries, q_local), jnp.float32),
        in_specs=[pl.BlockSpec(memory_space=pltpu.VMEM)] * (2 + len(blocks)),
        out_specs=pl.BlockSpec(memory_space=pltpu.VMEM),
        scratch_shapes=[pltpu.VMEM((waves * entries, 2 * q_local), jnp.float32)],
        name="product",
    )(tables, energy, *blocks)


def direct(blk, wide, coupling, rp_cells, re_cells, q_points, k_points, mode_energy):
    slab, cells, _, total = coupling.shape
    entries = total // wide
    waves = k_points.shape[1]
    unit = slab // sum(SHARES)
    starts = []
    for share in SHARES:
        starts.append((sum(r for _, r in starts), share * unit))

    turn = jnp.mod(
        jnp.sum(re_cells[:, :, None] * k_points[:, None, :], axis=0), MESHK
    )
    tail = jnp.broadcast_to(
        turn.astype(coupling.dtype)[None, :, :, None], (TAIL, cells, waves, entries)
    )
    steps = tuple(range(wide - 1, -1, -1))
    cuts = cut(coupling, tail, starts, steps, entries)
    tables = table(rp_cells, q_points, starts, slab)

    moved = []
    for i, block in enumerate(cuts):
        step = steps[i % len(steps)]
        moved.append(swap(block, "wide", wide, step) if step else block)
    blocks, pieces = [], []
    row = 0
    for c, (_, rows) in enumerate(starts):
        group = moved[c * len(steps) : (c + 1) * len(steps)]
        mine = combine(group, rows, cells, entries, waves)
        held = {0: mine}
        for step in range(blk - 2, 0, -2):
            held[step] = swap(mine, "blk", blk, step)
        for step in list(held):
            held[step + 1] = swap(held[step], "blk", blk, 1)
        for step, value in held.items():
            blocks.append(value)
            pieces.append((step, row, 2 * rows))
        row += 2 * rows
    return product(tables, mode_energy, blocks, pieces, waves, entries)


def phase_parts(left, right, modulus):
    whole = jnp.sum(left[:, :, None] * right[:, None, :], axis=0)
    angle = jnp.mod(whole, modulus).astype(jnp.float32) * (2.0 * math.pi / modulus)
    return (jnp.cos(angle), jnp.sin(angle))


def general(coupling, rp_cells, re_cells, q_points, k_points, mode_energy):
    moved = lax.all_to_all(coupling, "wide", split_axis=3, concat_axis=1, tiled=True)
    cells = lax.all_gather(re_cells, "wide", axis=1, tiled=True)
    entries = moved.shape[3]
    offset = lax.axis_index("wide") * entries
    k_cos, k_sin = phase_parts(k_points, cells, MESHK)
    real = moved[:, :, 0].astype(jnp.float32)
    imag = moved[:, :, 1].astype(jnp.float32)
    high = lax.Precision.HIGHEST
    turn = functools.partial(jnp.einsum, "kr,pre->pke", precision=high)
    held = jnp.stack(
        [turn(k_cos, real) - turn(k_sin, imag), turn(k_cos, imag) + turn(k_sin, real)],
        axis=2,
    ).astype(coupling.dtype)
    full = lax.all_gather(held, "blk", axis=0, tiled=True)
    cosine, sine = phase_parts(q_points, rp_cells, MESHQ)
    dot = functools.partial(
        jnp.einsum, "qp,pkse->skeq", preferred_element_type=jnp.float32
    )
    with_cos = dot(cosine.astype(full.dtype), full)
    with_sin = dot(sine.astype(full.dtype), full)
    index = (offset + jnp.arange(entries, dtype=jnp.int32)) % MODES
    weight = (1.0 / jnp.sqrt(2.0 * mode_energy))[index]
    return jnp.stack(
        [(with_cos[0] - with_sin[1]) * weight, (with_cos[1] + with_sin[0]) * weight],
        axis=1,
    )


def solution(mesh):
    blk, wide = mesh.shape["blk"], mesh.shape["wide"]

    def on_device(coupling, rp_cells, re_cells, q_points, k_points, mode_energy):
        args = (coupling, rp_cells, re_cells, q_points, k_points, mode_energy)
        slab, cells, _, total = coupling.shape
        waves = k_points.shape[1]
        fits = (
            blk & (blk - 1) == 0
            and wide & (wide - 1) == 0
            and blk > 1
            and total // wide == LANES
            and cells == 2
            and waves == 2
            and slab % 128 == 0
            and q_points.shape[1] % LANES == 0
        )
        return direct(blk, wide, *args) if fits else general(*args)

    in_specs = (
        P("blk", "wide", None, None),
        P(),
        P(None, "wide"),
        P(None, "blk"),
        P(),
        P(None, "blk"),
    )
    out_specs = P(None, None, "wide", "blk")
    return jax.shard_map(
        on_device, mesh=mesh, in_specs=in_specs, out_specs=out_specs, check_vma=False
    )
```

time: 107 us -> 60 us (0.56)
  blocking collectives: 29.7 us -> 0 us
  Pallas kernels: 0 us -> 26.7 us
  local copies, waits for them, and re-layouts: 24.1 us -> 3.92 us
  between operations: 13.6 us -> 0.11 us
  matrix products: 12 us -> 0 us
  starting transfers between devices: 0.04 us -> 9.78 us
  waiting for transfers between devices: 22.4 us -> 17 us
  other arithmetic: 4.91 us -> 2.26 us
    pallas_call x0 -> x4, Pallas kernels: none -> 26.7 us  [the longest x1 17.5 us: cut(): pl.pallas_call(functools.partial(slice_kernel, starts, steps, entries), o...]
    all_gather x1 -> x0, waiting for transfers between devices: 22.4 us -> none  [on_device(): lax.all_gather(flat, 'blk', axis=0, tiled=True)]
    all_to_all x1 -> x0, blocking collectives: 20.6 us -> none  [on_device(): lax.all_to_all(coupling, 'wide', split_axis=3, concat_axis=1, tiled=True)]
    ppermute x0 -> x10, waiting for transfers between devices: none -> 17 us  [swap(): return lax.ppermute(value, axis, xor_pairs(count, step))]
    dot_general x6 -> x0, matrix products: 12 us -> none  [the longest x1 6.53 us: on_device(): lax.dot_general(lax.all_gather(flat, 'blk', axis=0, tiled=True), table, (...]
    ppermute x0 -> x10, starting transfers between devices: none -> 9.78 us  [swap(): return lax.ppermute(value, axis, xor_pairs(count, step))]
    all_gather x1 -> x0, blocking collectives: 9.04 us -> none  [on_device(): cells = lax.all_gather(re_cells, 'wide', axis=1, tiled=True)]
    slice x1 -> x0, local copies, waits for them, and re-layouts: 8.14 us -> none  [on_device(): real = summed[:, 0, :, 0] - summed[:, 1, :, 1]]
  transfers between devices with their start and end apart: 1 -> 10, of which waited for: 1 -> 4; matrix products, arithmetic and copies ran while one was open for 5% -> 4% of each run, Pallas kernels for 0% -> 6%
where the time goes in v1:
time: 60 us; the launch traced here: 59.7 us
  Pallas kernels  26.7 us (44%)
  waiting for transfers between devices  17 us (28%)
  starting transfers between devices  9.78 us (16%)
  local copies, waits for them, and re-layouts  3.92 us (7%)
  other arithmetic  2.26 us (4%)
    pallas_call x1, Pallas kernels, cut(): pl.pallas_call(functools.partial(slice_kernel, starts, steps, entries), o...  17.5 us
    ppermute x10, waiting for transfers between devices, swap(): return lax.ppermute(value, axis, xor_pairs(count, step))  17 us
    ppermute x10, starting transfers between devices, swap(): return lax.ppermute(value, axis, xor_pairs(count, step))  9.78 us
    pallas_call x1, Pallas kernels, table(): pl.pallas_call(functools.partial(table_kernel, starts, slab), out_shape=j...  3.52 us
    pallas_call x1, Pallas kernels, product(): pl.pallas_call(functools.partial(product_kernel, pieces, waves, entries),...  3.43 us
    pallas_call x1, Pallas kernels, combine(): pl.pallas_call(functools.partial(combine_kernel, rows, cells, entries, wa...  2.16 us
    unnamed x20, local copies, waits for them, and re-layouts  2.04 us
  transfers between devices with their start and end apart: 10, of which 4 were waited for; matrix products, arithmetic and copies ran while one was open for 4% of the time, Pallas kernels for 6%

profile of v1, /device:TPU:0, one launch (start us, length us, event | category | flops | bytes accessed | tf_op | source)
XLA Modules:
  0.0 59.7 jit_solution(13815099279027417700)
XLA Ops:
  0.0 0.8 %multiply_reduce_fusion = s32[2,2]{1,0:T(2,128)S(1)} fusion(s32[3,2]{0,1:T(2,128)} %param.10, s32[3,2]{0,1:T(2,128)} %param.8), kind=kLoop, calls=%fused_computation.2 | loop fusion | flops 20 | bytes 64 | tf_op jit(solution)/shard_map/reduce_sum | solution.py:237
  0.9 0.7 %broadcast_in_dim.2.tail_ref = bf16[4,2,2,128]{3,2,1,0:T(2,128)(2,1)} broadcast(bf16[2,2]{1,0:T(2,128)(2,1)S(1)} %fusion.1), dimensions={1,2} | broadcast | bytes 4104 | tf_op jit(solution)/shard_map/broadcast_in_dim | solution.py:239
  1.5 17.5 %cut.1 = (bf16[132,2,2,128]{3,2,1,0:T(2,128)(2,1)}, bf16[132,2,2,128]{3,2,1,0:T(2,128)(2,1)}, bf16[132,2,2,128]{3,2,1,0:T(2,128)(2,1)}, bf16[132,2,2,128]{3,2,1,0:T(2,128)(2,1)}) custom-call(bf16[128,2,2,512]{3,2,1,0:T(2,128)(2,1)} %x_ref.1, bf16[4,2,2,128]{3,2,1,0:T(2,128)(2,1)} %broadcast_in_dim.2.tail_ref), custom_call_target="tpu_custom_call" | custom-call | tf_op jit(solution)/shard_map/cut/pallas_call | solution.py:62
  19.1 5.1 %collective-permute-start = (bf16[132,2,2,128]{3,2,1,0:T(2,128)(2,1)}, bf16[132,2,2,128]{3,2,1,0:T(2,128)(2,1)S(1)}, u32[]{:S(2)}, u32[]{:S(2)}) collective-permute-start(bf16[132,2,2,128]{3,2,1,0:T(2,128)(2,1)} %get-tuple-element.9), channel_id=1, source_target_pairs={{0,3},{1,2},{2,1},{3,0},{4,7},{5,6},{6,5},{7,4},{8,11},{9,10},{10,... | collective-permute-start | bytes 405512 | tf_op jit(solution)/shard_map/ppermute | solution.py:24
  24.2 0.0 collective-permute-start.1
  24.2 0.6 %collective-permute-start.2 = (bf16[132,2,2,128]{3,2,1,0:T(2,128)(2,1)}, bf16[132,2,2,128]{3,2,1,0:T(2,128)(2,1)S(1)}, u32[]{:S(2)}, u32[]{:S(2)}) collective-permute-start(bf16[132,2,2,128]{3,2,1,0:T(2,128)(2,1)} %get-tuple-element.11), channel_id=1, source_target_pairs={{0,1},{1,0},{2,3},{3,2},{4,5},{5,4},{6,7},{7,6},{8,9},{9,8},{10,11... | collective-permute-start | bytes 405512 | tf_op jit(solution)/shard_map/ppermute | solution.py:24
  24.9 4.1 %collective-permute-done = bf16[132,2,2,128]{3,2,1,0:T(2,128)(2,1)S(1)} collective-permute-done((bf16[132,2,2,128]{3,2,1,0:T(2,128)(2,1)}, bf16[132,2,2,128]{3,2,1,0:T(2,128)(2,1)S(1)}, u32[]{:S(2)}, u32[]{:S(2)}) %collective-permute-start) | collective-permute-done | bytes 135200 | tf_op jit(solution)/shard_map/ppermute | solution.py:24
  29.0 6.9 %collective-permute-done.1 = bf16[132,2,2,128]{3,2,1,0:T(2,128)(2,1)S(1)} collective-permute-done((bf16[132,2,2,128]{3,2,1,0:T(2,128)(2,1)}, bf16[132,2,2,128]{3,2,1,0:T(2,128)(2,1)S(1)}, u32[]{:S(2)}, u32[]{:S(2)}) %collective-permute-start.1) | collective-permute-done | bytes 135200 | tf_op jit(solution)/shard_map/ppermute | solution.py:24
  35.8 0.0 collective-permute-done.2
  35.9 0.6 %copy-done.1 = bf16[132,2,2,128]{3,2,1,0:T(2,128)(2,1)} copy-done((bf16[132,2,2,128]{3,2,1,0:T(2,128)(2,1)}, bf16[132,2,2,128]{3,2,1,0:T(2,128)(2,1)S(1)}, u32[]{:S(2)}) %copy-start.1) | copy-done | bytes 135192
  36.5 0.1 copy-done.2
  36.6 2.2 %combine.1.refs_0_ = bf16[256,256]{1,0:T(8,128)(2,1)} custom-call(bf16[528,128]{1,0:T(8,128)(2,1)} %bitcast.5, bf16[528,128]{1,0:T(8,128)(2,1)} %bitcast.6, bf16[528,128]{1,0:T(8,128)(2,1)} %bitcast.7, bf16[528,128]{1,0:T(8,128)(2,1)} %bitcast.4), custom_call_target="tpu_custom_call" | custom-call | tf_op jit(solution)/shard_map/combine/pallas_call | solution.py:108
  38.7 1.5 %collective-permute-start.5 = (bf16[256,256]{1,0:T(8,128)(2,1)}, bf16[256,256]{1,0:T(8,128)(2,1)S(1)}, u32[]{:S(2)}, u32[]{:S(2)}) collective-permute-start(bf16[256,256]{1,0:T(8,128)(2,1)} %combine.1.refs_0_), channel_id=1, source_target_pairs={{0,8},{4,12},{8,0},{12,4},{16,24},{20,28},{24,16},{28,20},{1,9},{5... | collective-permute-start | bytes 393224 | tf_op jit(solution)/shard_map/ppermute | solution.py:24
  40.2 1.5 %collective-permute-start.4 = (bf16[256,256]{1,0:T(8,128)(2,1)}, bf16[256,256]{1,0:T(8,128)(2,1)S(1)}, u32[]{:S(2)}, u32[]{:S(2)}) collective-permute-start(bf16[256,256]{1,0:T(8,128)(2,1)} %combine.1.refs_0_), channel_id=1, source_target_pairs={{0,16},{4,20},{8,24},{12,28},{16,0},{20,4},{24,8},{28,12},{1,17},{... | collective-permute-start | bytes 393224 | tf_op jit(solution)/shard_map/ppermute | solution.py:24
  41.7 0.5 collective-permute-start.3
  42.2 0.0 collective-permute-start.6
  42.2 2.5 %collective-permute-done.5.refs_3_ = bf16[256,256]{1,0:T(8,128)(2,1)S(1)} collective-permute-done((bf16[256,256]{1,0:T(8,128)(2,1)}, bf16[256,256]{1,0:T(8,128)(2,1)S(1)}, u32[]{:S(2)}, u32[]{:S(2)}) %collective-permute-start.5) | collective-permute-done | bytes 131104 | tf_op jit(solution)/shard_map/ppermute | solution.py:24
  44.7 3.5 %collective-permute-done.4.refs_2_ = bf16[256,256]{1,0:T(8,128)(2,1)S(1)} collective-permute-done((bf16[256,256]{1,0:T(8,128)(2,1)}, bf16[256,256]{1,0:T(8,128)(2,1)S(1)}, u32[]{:S(2)}, u32[]{:S(2)}) %collective-permute-start.4) | collective-permute-done | bytes 131104 | tf_op jit(solution)/shard_map/ppermute | solution.py:24
  48.2 0.5 collective-permute-start.7
  48.7 0.7 %convert_element_type.18 = bf16[3,256]{1,0:T(4,128)(2,1)S(1)} convert(s32[3,256]{1,0:T(4,128)} %param.9) | non-fusion elementwise | flops 768 | bytes 4608 | tf_op jit(solution)/shard_map/convert_element_type | solution.py:175
  49.4 0.7 %convert_element_type.17 = bf16[3,1024]{1,0:T(4,128)(2,1)S(1)} convert(s32[3,1024]{1,0:T(4,128)} %param.7) | non-fusion elementwise | flops 3072 | bytes 18432 | tf_op jit(solution)/shard_map/convert_element_type | solution.py:174
  50.1 0.6 %pad.9.q_ref = bf16[16,256]{1,0:T(8,128)(2,1)} pad(bf16[3,256]{1,0:T(4,128)(2,1)S(1)} %convert_element_type.18, bf16[]{:T(256)} %constant.14.clone.1), padding=0_13x0_0 | pad | bytes 9730 | tf_op jit(solution)/shard_map/jit(_pad)/pad | solution.py:175
  50.7 0.6 %pad.8.rp_ref = bf16[16,1024]{1,0:T(8,128)(2,1)} pad(bf16[3,1024]{1,0:T(4,128)(2,1)S(1)} %convert_element_type.17, bf16[]{:T(256)} %constant.14.clone.1), padding=0_13x0_0 | pad | bytes 38914 | tf_op jit(solution)/shard_map/jit(_pad)/pad | solution.py:174
  51.3 3.5 %table.1.table_ref = bf16[8,256,512]{2,1,0:T(8,128)(2,1)} custom-call(bf16[16,1024]{1,0:T(8,128)(2,1)} %pad.8.rp_ref, bf16[16,256]{1,0:T(8,128)(2,1)} %pad.9.q_ref), custom_call_target="tpu_custom_call" | custom-call | flops 20971520 | bytes 2097152 | tf_op jit(solution)/shard_map/table/pallas_call | solution.py:176
  54.9 0.0 collective-permute-done.6.refs_4_
  54.9 0.0 collective-permute-done.9.refs_7_
  54.9 0.0 collective-permute-done.7.refs_5_
  54.9 0.6 copy-done.6
  55.5 0.1 copy-done.7
  55.6 0.0 copy-done.8
  55.6 0.7 %copy-done.9 = bf16[256,256]{1,0:T(8,128)(2,1)} copy-done((bf16[256,256]{1,0:T(8,128)(2,1)}, bf16[256,256]{1,0:T(8,128)(2,1)S(1)}, u32[]{:S(2)}) %copy-start.9) | copy-done | bytes 131096
  56.3 3.4 %product.1 = f32[2,2,128,256]{3,2,1,0:T(8,128)} custom-call(bf16[8,256,512]{2,1,0:T(8,128)(2,1)} %table.1.table_ref, f32[16,256]{1,0:T(8,128)} %energy_ref.1, bf16[256,256]{1,0:T(8,128)(2,1)} %combine.1.refs_0_, bf16[256,256]{1,0:T(8,128)(2,1)} %copy-done.5, bf16[256,256]{1,0:T(8,128)(2,1)} %copy-done.4, bf16[256,256]{1,0:T(8,128)(2,1)} %copy-done.3, ...), custom_call_target="tpu_custom_call" | custom-call | tf_op jit(solution)/shard_map/product/pallas_call | solution.py:217
  (19 shorter events, 0.0 us)
Async XLA Ops:
  19.1 9.9 %collective-permute-start = (bf16[132,2,2,128]{3,2,1,0:T(2,128)(2,1)}, bf16[132,2,2,128]{3,2,1,0:T(2,128)(2,1)S(1)}, u32[]{:S(2)}, u32[]{:S(2)}) collective-permute-start(bf16[132,2,2,128]{3,2,1,0:T(2,128)(2,1)} %get-tuple-element.9), channel_id=1, source_target_pairs={{0,3},{1,2},{2,1},{3,0},{4,7},{5,6},{6,5},{7,4},{8,11},{9,10},{10,... | collective-permute-start | bytes 405512 | tf_op jit(solution)/shard_map/ppermute | solution.py:24
  24.2 11.6 %collective-permute-start.1 = (bf16[132,2,2,128]{3,2,1,0:T(2,128)(2,1)}, bf16[132,2,2,128]{3,2,1,0:T(2,128)(2,1)S(1)}, u32[]{:S(2)}, u32[]{:S(2)}) collective-permute-start(bf16[132,2,2,128]{3,2,1,0:T(2,128)(2,1)} %get-tuple-element.10), channel_id=1, source_target_pairs={{0,2},{1,3},{2,0},{3,1},{4,6},{5,7},{6,4},{7,5},{8,10},{9,11},{10,... | collective-permute-start | bytes 405512 | tf_op jit(solution)/shard_map/ppermute | solution.py:24
  24.2 11.6 %collective-permute-start.2 = (bf16[132,2,2,128]{3,2,1,0:T(2,128)(2,1)}, bf16[132,2,2,128]{3,2,1,0:T(2,128)(2,1)S(1)}, u32[]{:S(2)}, u32[]{:S(2)}) collective-permute-start(bf16[132,2,2,128]{3,2,1,0:T(2,128)(2,1)} %get-tuple-element.11), channel_id=1, source_target_pairs={{0,1},{1,0},{2,3},{3,2},{4,5},{5,4},{6,7},{7,6},{8,9},{9,8},{10,11... | collective-permute-start | bytes 405512 | tf_op jit(solution)/shard_map/ppermute | solution.py:24
  29.0 6.9 %copy-start = (bf16[132,2,2,128]{3,2,1,0:T(2,128)(2,1)}, bf16[132,2,2,128]{3,2,1,0:T(2,128)(2,1)S(1)}, u32[]{:S(2)}) copy-start(bf16[132,2,2,128]{3,2,1,0:T(2,128)(2,1)S(1)} %collective-permute-done) | copy-start | bytes 405508
  35.8 0.7 %copy-start.1 = (bf16[132,2,2,128]{3,2,1,0:T(2,128)(2,1)}, bf16[132,2,2,128]{3,2,1,0:T(2,128)(2,1)S(1)}, u32[]{:S(2)}) copy-start(bf16[132,2,2,128]{3,2,1,0:T(2,128)(2,1)S(1)} %collective-permute-done.1) | copy-start | bytes 405508
  35.9 0.7 %copy-start.2 = (bf16[132,2,2,128]{3,2,1,0:T(2,128)(2,1)}, bf16[132,2,2,128]{3,2,1,0:T(2,128)(2,1)S(1)}, u32[]{:S(2)}) copy-start(bf16[132,2,2,128]{3,2,1,0:T(2,128)(2,1)S(1)} %collective-permute-done.2) | copy-start | bytes 405508
  38.7 6.0 %collective-permute-start.5 = (bf16[256,256]{1,0:T(8,128)(2,1)}, bf16[256,256]{1,0:T(8,128)(2,1)S(1)}, u32[]{:S(2)}, u32[]{:S(2)}) collective-permute-start(bf16[256,256]{1,0:T(8,128)(2,1)} %combine.1.refs_0_), channel_id=1, source_target_pairs={{0,8},{4,12},{8,0},{12,4},{16,24},{20,28},{24,16},{28,20},{1,9},{5... | collective-permute-start | bytes 393224 | tf_op jit(solution)/shard_map/ppermute | solution.py:24
  40.2 8.0 %collective-permute-start.4 = (bf16[256,256]{1,0:T(8,128)(2,1)}, bf16[256,256]{1,0:T(8,128)(2,1)S(1)}, u32[]{:S(2)}, u32[]{:S(2)}) collective-permute-start(bf16[256,256]{1,0:T(8,128)(2,1)} %combine.1.refs_0_), channel_id=1, source_target_pairs={{0,16},{4,20},{8,24},{12,28},{16,0},{20,4},{24,8},{28,12},{1,17},{... | collective-permute-start | bytes 393224 | tf_op jit(solution)/shard_map/ppermute | solution.py:24
  41.7 6.5 %collective-permute-start.3 = (bf16[256,256]{1,0:T(8,128)(2,1)}, bf16[256,256]{1,0:T(8,128)(2,1)S(1)}, u32[]{:S(2)}, u32[]{:S(2)}) collective-permute-start(bf16[256,256]{1,0:T(8,128)(2,1)} %combine.1.refs_0_), channel_id=1, source_target_pairs={{0,24},{4,28},{8,16},{12,20},{16,8},{20,12},{24,0},{28,4},{1,25},{... | collective-permute-start | bytes 393224 | tf_op jit(solution)/shard_map/ppermute | solution.py:24
  42.2 12.7 %collective-permute-start.6 = (bf16[256,256]{1,0:T(8,128)(2,1)}, bf16[256,256]{1,0:T(8,128)(2,1)S(1)}, u32[]{:S(2)}, u32[]{:S(2)}) collective-permute-start(bf16[256,256]{1,0:T(8,128)(2,1)} %combine.1.refs_0_), channel_id=1, source_target_pairs={{0,4},{4,0},{8,12},{12,8},{16,20},{20,16},{24,28},{28,24},{1,5},{5... | collective-permute-start | bytes 393224 | tf_op jit(solution)/shard_map/ppermute | solution.py:24
  44.7 10.2 %copy-start.3 = (bf16[256,256]{1,0:T(8,128)(2,1)}, bf16[256,256]{1,0:T(8,128)(2,1)S(1)}, u32[]{:S(2)}) copy-start(bf16[256,256]{1,0:T(8,128)(2,1)S(1)} %collective-permute-done.5.refs_3_) | copy-start | bytes 393220
  44.7 10.2 %collective-permute-start.9 = (bf16[256,256]{1,0:T(8,128)(2,1)S(1)}, bf16[256,256]{1,0:T(8,128)(2,1)S(1)}, u32[]{:S(2)}, u32[]{:S(2)}) collective-permute-start(bf16[256,256]{1,0:T(8,128)(2,1)S(1)} %collective-permute-done.5.refs_3_), channel_id=1, source_target_pairs={{0,4},{4,0},{8,12},{12,8},{16,20},{20,16},{24,28},{28,24},{1,5},{5... | collective-permute-start | bytes 393224 | tf_op jit(solution)/shard_map/ppermute | solution.py:24
  48.2 6.7 %copy-start.4 = (bf16[256,256]{1,0:T(8,128)(2,1)}, bf16[256,256]{1,0:T(8,128)(2,1)S(1)}, u32[]{:S(2)}) copy-start(bf16[256,256]{1,0:T(8,128)(2,1)S(1)} %collective-permute-done.4.refs_2_) | copy-start | bytes 393220
  48.2 6.7 %collective-permute-start.8 = (bf16[256,256]{1,0:T(8,128)(2,1)S(1)}, bf16[256,256]{1,0:T(8,128)(2,1)S(1)}, u32[]{:S(2)}, u32[]{:S(2)}) collective-permute-start(bf16[256,256]{1,0:T(8,128)(2,1)S(1)} %collective-permute-done.4.refs_2_), channel_id=1, source_target_pairs={{0,4},{4,0},{8,12},{12,8},{16,20},{20,16},{24,28},{28,24},{1,5},{5... | collective-permute-start | bytes 393224 | tf_op jit(solution)/shard_map/ppermute | solution.py:24
  48.2 6.7 %copy-start.5 = (bf16[256,256]{1,0:T(8,128)(2,1)}, bf16[256,256]{1,0:T(8,128)(2,1)S(1)}, u32[]{:S(2)}) copy-start(bf16[256,256]{1,0:T(8,128)(2,1)S(1)} %collective-permute-done.3.refs_1_) | copy-start | bytes 393220
  48.2 6.7 %collective-permute-start.7 = (bf16[256,256]{1,0:T(8,128)(2,1)S(1)}, bf16[256,256]{1,0:T(8,128)(2,1)S(1)}, u32[]{:S(2)}, u32[]{:S(2)}) collective-permute-start(bf16[256,256]{1,0:T(8,128)(2,1)S(1)} %collective-permute-done.3.refs_1_), channel_id=1, source_target_pairs={{0,4},{4,0},{8,12},{12,8},{16,20},{20,16},{24,28},{28,24},{1,5},{5... | collective-permute-start | bytes 393224 | tf_op jit(solution)/shard_map/ppermute | solution.py:24
  54.9 0.7 %copy-start.6 = (bf16[256,256]{1,0:T(8,128)(2,1)}, bf16[256,256]{1,0:T(8,128)(2,1)S(1)}, u32[]{:S(2)}) copy-start(bf16[256,256]{1,0:T(8,128)(2,1)S(1)} %collective-permute-done.6.refs_4_) | copy-start | bytes 393220
  54.9 0.7 %copy-start.7 = (bf16[256,256]{1,0:T(8,128)(2,1)}, bf16[256,256]{1,0:T(8,128)(2,1)S(1)}, u32[]{:S(2)}) copy-start(bf16[256,256]{1,0:T(8,128)(2,1)S(1)} %collective-permute-done.9.refs_7_) | copy-start | bytes 393220
  54.9 0.7 %copy-start.8 = (bf16[256,256]{1,0:T(8,128)(2,1)}, bf16[256,256]{1,0:T(8,128)(2,1)S(1)}, u32[]{:S(2)}) copy-start(bf16[256,256]{1,0:T(8,128)(2,1)S(1)} %collective-permute-done.8.refs_6_) | copy-start | bytes 393220
  55.6 0.7 %copy-start.9 = (bf16[256,256]{1,0:T(8,128)(2,1)}, bf16[256,256]{1,0:T(8,128)(2,1)S(1)}, u32[]{:S(2)}) copy-start(bf16[256,256]{1,0:T(8,128)(2,1)S(1)} %collective-permute-done.7.refs_5_) | copy-start | bytes 393220

commit v2 on v1

v2 whole, which is shorter than its diff:
```python
import functools
import math

import jax
import jax.numpy as jnp
from jax import lax
from jax.experimental import pallas as pl
from jax.experimental.pallas import tpu as pltpu
from jax.sharding import PartitionSpec as P


MODES = 16
MESHQ = 32
MESHK = 32
LANES = 128
TAIL = 4
SHARES = (1,)
LATE = 2


def xor_pairs(count, step):
    return [(i, i ^ step) for i in range(count)]


def swap(value, axis, count, step):
    return lax.ppermute(value, axis, xor_pairs(count, step))


def grant(mebibytes):
    return pltpu.CompilerParams(vmem_limit_bytes=int(mebibytes * 2**20))


def cut_kernel(starts, steps, entries, x_ref, cells_ref, points_ref, *rest):
    outs = rest[:-4]
    cells, points, sem, small = rest[-4:]
    me = lax.axis_index("wide")
    copies = [
        pltpu.make_async_copy(cells_ref, cells, small.at[0]),
        pltpu.make_async_copy(points_ref, points, small.at[1]),
    ]
    for c, (first, rows) in enumerate(starts):
        for j, step in enumerate(steps):
            i = c * len(steps) + j
            column = pl.multiple_of((me ^ step) * entries, LANES)
            copies.append(
                pltpu.make_async_copy(
                    x_ref.at[pl.ds(first, rows), :, :, pl.ds(column, entries)],
                    outs[i].at[pl.ds(0, rows)],
                    sem.at[i],
                )
            )
    for copy in copies:
        copy.start()
    for copy in copies[:2]:
        copy.wait()
    shape = (TAIL,) + outs[0].shape[1:]
    which_cell = lax.broadcasted_iota(jnp.int32, shape, 1)
    which_wave = lax.broadcasted_iota(jnp.int32, shape, 2)
    tail = jnp.zeros(shape, jnp.float32)
    for r in range(cells.shape[0]):
        for k in range(points.shape[0]):
            turn = cells[r, 0] * points[k, 0]
            for axis in range(1, cells.shape[1]):
                turn += cells[r, axis] * points[k, axis]
            turn = lax.rem(lax.rem(turn, MESHK) + MESHK, MESHK)
            here = (which_cell == r) & (which_wave == k)
            tail = jnp.where(here, turn.astype(jnp.float32), tail)
    tail = tail.astype(outs[0].dtype)
    for i, out in enumerate(outs):
        rows = starts[i // len(steps)][1]
        out[pl.ds(rows, TAIL)] = tail
    for copy in copies[2:]:
        copy.wait()


def cut(coupling, re_cells, k_points, starts, steps, entries):
    cells = coupling.shape[1]
    shapes = []
    for _, rows in starts:
        for _ in steps:
            shapes.append(
                jax.ShapeDtypeStruct((rows + TAIL, cells, 2, entries), coupling.dtype)
            )
    return pl.pallas_call(
        functools.partial(cut_kernel, starts, steps, entries),
        out_shape=shapes,
        in_specs=[pl.BlockSpec(memory_space=pl.ANY)] * 3,
        out_specs=[pl.BlockSpec(memory_space=pltpu.VMEM)] * len(shapes),
        scratch_shapes=[
            pltpu.SMEM(re_cells.shape[::-1], jnp.int32),
            pltpu.SMEM(k_points.shape[::-1], jnp.int32),
            pltpu.SemaphoreType.DMA((len(shapes),)),
            pltpu.SemaphoreType.DMA((2,)),
        ],
        compiler_params=grant(4),
        name="cut",
    )(coupling, re_cells.T, k_points.T)


def circle(modulus):
    lane = lax.broadcasted_iota(jnp.int32, (8, LANES), 1) % modulus
    angle = lane.astype(jnp.float32) * (2.0 * math.pi / modulus)
    return jnp.cos(angle), jnp.sin(angle)


def look(values, index):
    return jnp.take_along_axis(values, index, axis=1, mode="promise_in_bounds")


def combine_kernel(rows, cells, entries, waves, cos_ref, sin_ref, *refs):
    ins = refs[:-2]
    out, work = refs[-2], refs[-1]
    per = 2 * cells
    phases = []
    for i, ref in enumerate(ins):
        work[i] = ref[...].astype(jnp.float32)
    for i in range(len(ins)):
        turn = work[i, pl.ds(rows * per, 8), :].astype(jnp.int32)
        phases.append((look(cos_ref[...], turn), look(sin_ref[...], turn)))
    step = 32
    for first in range(0, rows, step):
        re = [None] * waves
        im = [None] * waves
        for i in range(len(ins)):
            cos, sin = phases[i]
            for r in range(cells):
                a = work[i, pl.ds(first * per + 2 * r, step, stride=per), :]
                b = work[i, pl.ds(first * per + 2 * r + 1, step, stride=per), :]
                for k in range(waves):
                    at = r * waves + k
                    c = cos[at : at + 1, :]
                    s = sin[at : at + 1, :]
                    x = c * a - s * b
                    y = c * b + s * a
                    re[k] = x if re[k] is None else re[k] + x
                    im[k] = y if im[k] is None else im[k] + y
        for k in range(waves):
            lanes = pl.ds(k * entries, entries)
            out[pl.ds(first, step), lanes] = re[k].astype(out.dtype)
            out[pl.ds(rows + first, step), lanes] = im[k].astype(out.dtype)


def combine(circles, blocks, rows, cells, entries, waves):
    flat = [b.reshape(b.shape[0] * 2 * cells, entries) for b in blocks]
    full = flat[0].shape[0]
    return pl.pallas_call(
        functools.partial(combine_kernel, rows, cells, entries, waves),
        out_shape=jax.ShapeDtypeStruct((2 * rows, waves * entries), jnp.bfloat16),
        in_specs=[pl.BlockSpec(memory_space=pltpu.VMEM)] * (2 + len(flat)),
        out_specs=pl.BlockSpec(memory_space=pltpu.VMEM),
        scratch_shapes=[pltpu.VMEM((len(flat), full, entries), jnp.float32)],
        compiler_params=grant(6),
        name="combine",
    )(*circles, *flat)


def table_kernel(starts, slab, rp_ref, q_ref, out_ref, cos_ref, sin_ref):
    cos_ref[...], sin_ref[...] = circle(MESHK)
    cos_table, sin_table = circle(MESHQ)
    blocks = out_ref.shape[0]
    q_local = q_ref.shape[1]
    step = 32
    q = q_ref[...].astype(jnp.bfloat16)
    for block in range(blocks):
        n = lax.dot_general(
            rp_ref[:, pl.ds(block * slab, slab)].astype(jnp.bfloat16),
            q,
            (((0,), (0,)), ((), ())),
            preferred_element_type=jnp.float32,
        )
        m = n - MESHQ * jnp.floor(n * (1.0 / MESHQ))
        index = m.astype(jnp.int32)
        row = 0
        for first, rows in starts:
            for top in range(first, first + rows, step):
                for left in range(0, q_local, LANES):
                    cos_rows = []
                    sin_rows = []
                    for sub in range(top, top + step, 8):
                        at = index[sub : sub + 8, left : left + LANES]
                        cos_rows.append(look(cos_table, at))
                        sin_rows.append(look(sin_table, at))
                    c = jnp.concatenate(cos_rows, axis=0).astype(jnp.bfloat16)
                    s = jnp.concatenate(sin_rows, axis=0).astype(jnp.bfloat16)
                    re_rows = pl.ds(row + top - first, step)
                    im_rows = pl.ds(row + rows + top - first, step)
                    near = pl.ds(left, LANES)
                    far = pl.ds(q_local + left, LANES)
                    out_ref[block, re_rows, near] = c
                    out_ref[block, re_rows, far] = s
                    out_ref[block, im_rows, near] = -s
                    out_ref[block, im_rows, far] = c
            row += 2 * rows


def table(rp_cells, q_points, starts, slab):
    blocks = rp_cells.shape[1] // slab
    q_local = q_points.shape[1]
    spot = jax.ShapeDtypeStruct((8, LANES), jnp.float32)
    return pl.pallas_call(
        functools.partial(table_kernel, starts, slab),
        out_shape=[
            jax.ShapeDtypeStruct((blocks, 2 * slab, 2 * q_local), jnp.bfloat16),
            spot,
            spot,
        ],
        in_specs=[pl.BlockSpec(memory_space=pltpu.VMEM)] * 2,
        out_specs=[pl.BlockSpec(memory_space=pltpu.VMEM)] * 3,
        compiler_params=grant(6),
        cost_estimate=pl.CostEstimate(
            flops=8 * blocks * slab * q_local * 10,
            bytes_accessed=blocks * slab * q_local * 8,
            transcendentals=0,
        ),
        name="table",
    )(rp_cells, q_points)


def partial_kernel(pieces, table_ref, *refs):
    ins, out = refs[:-1], refs[-1]
    me = lax.axis_index("blk")
    for i, (step, row, rows) in enumerate(pieces):
        part = lax.dot_general(
            ins[i][...],
            table_ref[me ^ step, pl.ds(row, rows), :],
            (((0,), (0,)), ((), ())),
            preferred_element_type=jnp.float32,
        )
        if i == 0:
            out[...] = part
        else:
            out[...] += part


def partial(tables, blocks, pieces):
    shape = (blocks[0].shape[1], tables.shape[2])
    depth = sum(piece[2] for piece in pieces)
    return pl.pallas_call(
        functools.partial(partial_kernel, pieces),
        out_shape=jax.ShapeDtypeStruct(shape, jnp.float32),
        in_specs=[pl.BlockSpec(memory_space=pltpu.VMEM)] * (1 + len(blocks)),
        out_specs=pl.BlockSpec(memory_space=pltpu.VMEM),
        compiler_params=grant(8),
        cost_estimate=pl.CostEstimate(
            flops=2 * depth * shape[0] * shape[1],
            bytes_accessed=4 * shape[0] * shape[1],
            transcendentals=0,
        ),
        name="partial",
    )(tables, *blocks)


def finish_kernel(pieces, waves, entries, table_ref, energy_ref, sum_ref, *refs):
    ins, out, held, sem = refs[:-3], refs[-3], refs[-2], refs[-1]
    me = lax.axis_index("blk")
    q_local = energy_ref.shape[1]
    weight = 1.0 / jnp.sqrt(2.0 * energy_ref[...])
    copies = []
    for k in range(waves):
        lanes = pl.ds(k * entries, entries)
        total = sum_ref[lanes, :]
        for i, (step, row, rows) in enumerate(pieces):
            total += lax.dot_general(
                ins[i][:, lanes],
                table_ref[me ^ step, pl.ds(row, rows), :],
                (((0,), (0,)), ((), ())),
                preferred_element_type=jnp.float32,
            )
        for part in range(2):
            for e in range(0, entries, MODES):
                held[k, part, pl.ds(e, MODES), :] = (
                    total[e : e + MODES, part * q_local : (part + 1) * q_local] * weight
                )
        copies.append(pltpu.make_async_copy(held.at[k], out.at[k], sem.at[k]))
        copies[-1].start()
    for copy in copies:
        copy.wait()


def finish(tables, energy, total, blocks, pieces, waves, entries):
    q_local = energy.shape[1]
    shape = (waves, 2, entries, q_local)
    return pl.pallas_call(
        functools.partial(finish_kernel, pieces, waves, entries),
        out_shape=jax.ShapeDtypeStruct(shape, jnp.float32),
        in_specs=[pl.BlockSpec(memory_space=pltpu.VMEM)] * (3 + len(blocks)),
        out_specs=pl.BlockSpec(memory_space=pl.ANY),
        scratch_shapes=[
            pltpu.VMEM(shape, jnp.float32),
            pltpu.SemaphoreType.DMA((waves,)),
        ],
        compiler_params=grant(8),
        name="finish",
    )(tables, energy, total, *blocks)


def direct(blk, wide, coupling, rp_cells, re_cells, q_points, k_points, mode_energy):
    slab, cells, _, total = coupling.shape
    entries = total // wide
    waves = k_points.shape[1]
    unit = slab // sum(SHARES)
    starts = []
    for share in SHARES:
        starts.append((sum(r for _, r in starts), share * unit))

    steps = tuple(range(wide - 1, -1, -1))
    cuts = cut(coupling, re_cells, k_points, starts, steps, entries)
    tables, *circles = table(rp_cells, q_points, starts, slab)

    moved = []
    for i, block in enumerate(cuts):
        step = steps[i % len(steps)]
        moved.append(swap(block, "wide", wide, step) if step else block)
    early, late = [], []
    row = 0
    for c, (_, rows) in enumerate(starts):
        group = moved[c * len(steps) : (c + 1) * len(steps)]
        mine = combine(circles, group, rows, cells, entries, waves)
        held = {0: mine}
        for step in range(blk - 2, 0, -2):
            held[step] = swap(mine, "blk", blk, step)
        for step in list(held):
            held[step + 1] = swap(held[step], "blk", blk, 1)
        for step, value in held.items():
            final = c == len(starts) - 1 and step >= LATE
            (late if final else early).append((value, (step, row, 2 * rows)))
        row += 2 * rows
    total = partial(tables, [v for v, _ in early], [p for _, p in early])
    return finish(
        tables,
        mode_energy,
        total,
        [v for v, _ in late],
        [p for _, p in late],
        waves,
        entries,
    )


def phase_parts(left, right, modulus):
    whole = jnp.sum(left[:, :, None] * right[:, None, :], axis=0)
    angle = jnp.mod(whole, modulus).astype(jnp.float32) * (2.0 * math.pi / modulus)
    return (jnp.cos(angle), jnp.sin(angle))


def general(coupling, rp_cells, re_cells, q_points, k_points, mode_energy):
    moved = lax.all_to_all(coupling, "wide", split_axis=3, concat_axis=1, tiled=True)
    cells = lax.all_gather(re_cells, "wide", axis=1, tiled=True)
    entries = moved.shape[3]
    offset = lax.axis_index("wide") * entries
    k_cos, k_sin = phase_parts(k_points, cells, MESHK)
    real = moved[:, :, 0].astype(jnp.float32)
    imag = moved[:, :, 1].astype(jnp.float32)
    high = lax.Precision.HIGHEST
    turn = functools.partial(jnp.einsum, "kr,pre->pke", precision=high)
    held = jnp.stack(
        [turn(k_cos, real) - turn(k_sin, imag), turn(k_cos, imag) + turn(k_sin, real)],
        axis=2,
    ).astype(coupling.dtype)
    full = lax.all_gather(held, "blk", axis=0, tiled=True)
    cosine, sine = phase_parts(q_points, rp_cells, MESHQ)
    dot = functools.partial(
        jnp.einsum, "qp,pkse->skeq", preferred_element_type=jnp.float32
    )
    with_cos = dot(cosine.astype(full.dtype), full)
    with_sin = dot(sine.astype(full.dtype), full)
    index = (offset + jnp.arange(entries, dtype=jnp.int32)) % MODES
    weight = (1.0 / jnp.sqrt(2.0 * mode_energy))[index]
    return jnp.stack(
        [(with_cos[0] - with_sin[1]) * weight, (with_cos[1] + with_sin[0]) * weight],
        axis=1,
    )


def solution(mesh):
    blk, wide = mesh.shape["blk"], mesh.shape["wide"]

    def on_device(coupling, rp_cells, re_cells, q_points, k_points, mode_energy):
        args = (coupling, rp_cells, re_cells, q_points, k_points, mode_energy)
        slab, cells, _, total = coupling.shape
        waves = k_points.shape[1]
        fits = (
            blk & (blk - 1) == 0
            and wide & (wide - 1) == 0
            and blk > 1
            and total // wide == LANES
            and cells == 2
            and waves == 2
            and slab % 128 == 0
            and q_points.shape[1] % LANES == 0
        )
        if not fits:
            return general(*args)
        return direct(blk, wide, *args)

    in_specs = (
        P("blk", "wide", None, None),
        P(),
        P(None, "wide"),
        P(None, "blk"),
        P(),
        P(None, "blk"),
    )
    out_specs = P(None, None, "wide", "blk")
    return jax.shard_map(
        on_device, mesh=mesh, in_specs=in_specs, out_specs=out_specs, check_vma=False
    )
```

time: 60 us -> 32.5 us (0.54)
  Pallas kernels: 26.7 us -> 3.56 us
  other arithmetic: 2.26 us -> 0 us
  waiting for transfers between devices: 17 us -> 14.9 us
    pallas_call x3 -> x4, Pallas kernels: 24.5 us -> 3.19 us  [the longest x1 1.33 us: finish(): pl.pallas_call(functools.partial(finish_kernel, pieces, waves, entries),...]
    ppermute x10, waiting for transfers between devices: 17 us -> 14.9 us  [swap(): return lax.ppermute(value, axis, xor_pairs(count, step))]
    pallas_call x1, Pallas kernels: 2.16 us -> 0.36 us  [combine(): pl.pallas_call(functools.partial(combine_kernel, rows, cells, entries, wa...]
    unnamed x20 -> x12, local copies, waits for them, and re-layouts: 2.04 us -> 3.8 us
    convert_element_type x3 -> x0, other arithmetic: 1.42 us -> none  [the longest x1 0.72 us: table(): rp = jnp.pad(rp_cells.astype(jnp.bfloat16), pad)]
    pad x2 -> x0, local copies, waits for them, and re-layouts: 1.22 us -> none  [the longest x1 0.62 us: table(): rp = jnp.pad(rp_cells.astype(jnp.bfloat16), pad)]
    reduce_sum x1 -> x0, other arithmetic: 0.84 us -> none  [direct(): jnp.sum(re_cells[:, :, None] * k_points[:, None, :], axis=0)]
    broadcast_in_dim x1 -> x0, local copies, waits for them, and re-layouts: 0.66 us -> none  [direct(): jnp.broadcast_to(turn.astype(coupling.dtype)[None, :, :, None], (TAIL, ce...]
  transfers between devices with their start and end apart: 10 -> 10, of which waited for: 4 -> 6; matrix products, arithmetic and copies ran while one was open for 4% -> 0% of each run, Pallas kernels for 6% -> 4%
where the time goes in v2:
time: 32.5 us; the launch traced here: 32.2 us
  waiting for transfers between devices  14.9 us (46%)
  starting transfers between devices  9.85 us (30%)
  local copies, waits for them, and re-layouts  3.8 us (12%)
  Pallas kernels  3.56 us (11%)
    ppermute x10, waiting for transfers between devices, swap(): return lax.ppermute(value, axis, xor_pairs(count, step))  14.9 us
    ppermute x10, starting transfers between devices, swap(): return lax.ppermute(value, axis, xor_pairs(count, step))  9.85 us
    unnamed x12, local copies, waits for them, and re-layouts  3.8 us
    pallas_call x1, Pallas kernels, finish(): pl.pallas_call(functools.partial(finish_kernel, pieces, waves, entries),...  1.33 us
    pallas_call x1, Pallas kernels, table(): pl.pallas_call(functools.partial(table_kernel, starts, slab), out_shape=[...  0.9 us
  transfers between devices with their start and end apart: 10, of which 6 were waited for; matrix products, arithmetic and copies ran while one was open for 0% of the time, Pallas kernels for 4%

profile of v2, /device:TPU:0, one launch (start us, length us, event | category | flops | bytes accessed | tf_op | source)
XLA Modules:
  0.0 32.2 jit_solution(16179706383540051615)
XLA Ops:
  0.0 0.0 copy-start
  0.0 1.0 %copy-done = bf16[128,2,2,512]{3,2,1,0:T(2,128)(2,1)S(1)} copy-done((bf16[128,2,2,512]{3,2,1,0:T(2,128)(2,1)S(1)}, bf16[128,2,2,512]{3,2,1,0:T(2,128)(2,1)}, u32[]{:S(2)}) %copy-start) | copy-done | bytes 524312
  1.0 0.7 %copy-done.2 = s32[3,2]{0,1:T(2,128)S(1)} copy-done((s32[3,2]{0,1:T(2,128)S(1)}, s32[3,2]{0,1:T(2,128)}, u32[]{:S(2)}) %copy-start.2) | copy-done | bytes 48
  1.7 0.7 %copy-done.3 = s32[3,2]{0,1:T(2,128)S(1)} copy-done((s32[3,2]{0,1:T(2,128)S(1)}, s32[3,2]{0,1:T(2,128)}, u32[]{:S(2)}) %copy-start.3) | copy-done | bytes 48
  2.4 0.6 %cut.1 = (bf16[132,2,2,128]{3,2,1,0:T(2,128)(2,1)S(1)}, bf16[132,2,2,128]{3,2,1,0:T(2,128)(2,1)S(1)}, bf16[132,2,2,128]{3,2,1,0:T(2,128)(2,1)S(1)}, bf16[132,2,2,128]{3,2,1,0:T(2,128)(2,1)S(1)}) custom-call(bf16[128,2,2,512]{3,2,1,0:T(2,128)(2,1)S(1)} %copy-done, s32[2,3]{1,0:T(2,128)S(1)} %bitcast.10, s32[2,3]{1,0:T(2,128)S(1)} %bitcast.11), custom_call_target="tpu_custom_call" | custom-call | tf_op jit(solution)/shard_map/cut/pallas_call | solution.py:84
  3.1 5.1 %collective-permute-start = (bf16[132,2,2,128]{3,2,1,0:T(2,128)(2,1)S(1)}, bf16[132,2,2,128]{3,2,1,0:T(2,128)(2,1)S(1)}, u32[]{:S(2)}, u32[]{:S(2)}) collective-permute-start(bf16[132,2,2,128]{3,2,1,0:T(2,128)(2,1)S(1)} %get-tuple-element.15), channel_id=1, source_target_pairs={{0,3},{1,2},{2,1},{3,0},{4,7},{5,6},{6,5},{7,4},{8,11},{9,10},{10,... | collective-permute-start | bytes 405512 | tf_op jit(solution)/shard_map/ppermute | solution.py:26
  8.2 0.0 collective-permute-start.1
  8.2 0.6 %collective-permute-start.2 = (bf16[132,2,2,128]{3,2,1,0:T(2,128)(2,1)S(1)}, bf16[132,2,2,128]{3,2,1,0:T(2,128)(2,1)S(1)}, u32[]{:S(2)}, u32[]{:S(2)}) collective-permute-start(bf16[132,2,2,128]{3,2,1,0:T(2,128)(2,1)S(1)} %get-tuple-element.17), channel_id=1, source_target_pairs={{0,1},{1,0},{2,3},{3,2},{4,5},{5,4},{6,7},{7,6},{8,9},{9,8},{10,11... | collective-permute-start | bytes 405512 | tf_op jit(solution)/shard_map/ppermute | solution.py:26
  8.8 0.7 %copy-done.4 = s32[3,1024]{1,0:T(4,128)S(1)} copy-done((s32[3,1024]{1,0:T(4,128)S(1)}, s32[3,1024]{1,0:T(4,128)}, u32[]{:S(2)}) %copy-start.4) | copy-done | bytes 12312
  9.6 0.7 %copy-done.5 = s32[3,256]{1,0:T(4,128)S(1)} copy-done((s32[3,256]{1,0:T(4,128)S(1)}, s32[3,256]{1,0:T(4,128)}, u32[]{:S(2)}) %copy-start.5) | copy-done | bytes 3096
  10.3 0.9 %table.1 = (bf16[8,256,512]{2,1,0:T(8,128)(2,1)S(1)}, f32[8,128]{1,0:T(8,128)S(1)}, f32[8,128]{1,0:T(8,128)S(1)}) custom-call(s32[3,1024]{1,0:T(4,128)S(1)} %copy-done.4, s32[3,256]{1,0:T(4,128)S(1)} %copy-done.5), custom_call_target="tpu_custom_call" | custom-call | flops 20971520 | bytes 2097152 | tf_op jit(solution)/shard_map/table/pallas_call | solution.py:200
  11.2 1.6 %collective-permute-done = bf16[132,2,2,128]{3,2,1,0:T(2,128)(2,1)S(1)} collective-permute-done((bf16[132,2,2,128]{3,2,1,0:T(2,128)(2,1)S(1)}, bf16[132,2,2,128]{3,2,1,0:T(2,128)(2,1)S(1)}, u32[]{:S(2)}, u32[]{:S(2)}) %collective-permute-start) | collective-permute-done | bytes 135200 | tf_op jit(solution)/shard_map/ppermute | solution.py:26
  12.7 6.9 %collective-permute-done.1 = bf16[132,2,2,128]{3,2,1,0:T(2,128)(2,1)S(1)} collective-permute-done((bf16[132,2,2,128]{3,2,1,0:T(2,128)(2,1)S(1)}, bf16[132,2,2,128]{3,2,1,0:T(2,128)(2,1)S(1)}, u32[]{:S(2)}, u32[]{:S(2)}) %collective-permute-start.1) | collective-permute-done | bytes 135200 | tf_op jit(solution)/shard_map/ppermute | solution.py:26
  19.6 0.0 collective-permute-done.2
  19.6 0.4 %combine.1.refs_0_ = bf16[256,256]{1,0:T(8,128)(2,1)S(1)} custom-call(f32[8,128]{1,0:T(8,128)S(1)} %get-tuple-element.13.cos_ref, f32[8,128]{1,0:T(8,128)S(1)} %get-tuple-element.14.sin_ref, bf16[528,128]{1,0:T(8,128)(2,1)S(1)} %bitcast.7, bf16[528,128]{1,0:T(8,128)(2,1)S(1)} %bitcast.8, bf16[528,128]{1,0:T(8,128)(2,1)S(1)} %bitcast.9, ...), custom_call_target="tpu_custom_call" | custom-call | tf_op jit(solution)/shard_map/combine/pallas_call | solution.py:146
  20.0 1.6 %collective-permute-start.6 = (bf16[256,256]{1,0:T(8,128)(2,1)S(1)}, bf16[256,256]{1,0:T(8,128)(2,1)S(1)}, u32[]{:S(2)}, u32[]{:S(2)}) collective-permute-start(bf16[256,256]{1,0:T(8,128)(2,1)S(1)} %combine.1.refs_0_), channel_id=1, source_target_pairs={{0,8},{4,12},{8,0},{12,4},{16,24},{20,28},{24,16},{28,20},{1,9},{5... | collective-permute-start | bytes 393224 | tf_op jit(solution)/shard_map/ppermute | solution.py:26
  21.6 1.5 %collective-permute-start.5 = (bf16[256,256]{1,0:T(8,128)(2,1)S(1)}, bf16[256,256]{1,0:T(8,128)(2,1)S(1)}, u32[]{:S(2)}, u32[]{:S(2)}) collective-permute-start(bf16[256,256]{1,0:T(8,128)(2,1)S(1)} %combine.1.refs_0_), channel_id=1, source_target_pairs={{0,16},{4,20},{8,24},{12,28},{16,0},{20,4},{24,8},{28,12},{1,17},{... | collective-permute-start | bytes 393224 | tf_op jit(solution)/shard_map/ppermute | solution.py:26
  23.1 0.5 %collective-permute-start.4 = (bf16[256,256]{1,0:T(8,128)(2,1)S(1)}, bf16[256,256]{1,0:T(8,128)(2,1)S(1)}, u32[]{:S(2)}, u32[]{:S(2)}) collective-permute-start(bf16[256,256]{1,0:T(8,128)(2,1)S(1)} %combine.1.refs_0_), channel_id=1, source_target_pairs={{0,24},{4,28},{8,16},{12,20},{16,8},{20,12},{24,0},{28,4},{1,25},{... | collective-permute-start | bytes 393224 | tf_op jit(solution)/shard_map/ppermute | solution.py:26
  23.6 0.0 collective-permute-start.3
  23.6 2.3 %collective-permute-done.6.refs_2_ = bf16[256,256]{1,0:T(8,128)(2,1)S(1)} collective-permute-done((bf16[256,256]{1,0:T(8,128)(2,1)S(1)}, bf16[256,256]{1,0:T(8,128)(2,1)S(1)}, u32[]{:S(2)}, u32[]{:S(2)}) %collective-permute-start.6) | collective-permute-done | bytes 131104 | tf_op jit(solution)/shard_map/ppermute | solution.py:26
  25.8 0.0 collective-permute-start.9
  25.8 3.5 %collective-permute-done.5.refs_1_ = bf16[256,256]{1,0:T(8,128)(2,1)S(1)} collective-permute-done((bf16[256,256]{1,0:T(8,128)(2,1)S(1)}, bf16[256,256]{1,0:T(8,128)(2,1)S(1)}, u32[]{:S(2)}, u32[]{:S(2)}) %collective-permute-start.5) | collective-permute-done | bytes 131104 | tf_op jit(solution)/shard_map/ppermute | solution.py:26
  29.3 0.0 collective-permute-start.8
  29.3 0.0 collective-permute-done.4.refs_0_
  29.3 0.5 %collective-permute-start.7 = (bf16[256,256]{1,0:T(8,128)(2,1)S(1)}, bf16[256,256]{1,0:T(8,128)(2,1)S(1)}, u32[]{:S(2)}, u32[]{:S(2)}) collective-permute-start(bf16[256,256]{1,0:T(8,128)(2,1)S(1)} %collective-permute-done.4.refs_0_), channel_id=1, source_target_pairs={{0,4},{4,0},{8,12},{12,8},{16,20},{20,16},{24,28},{28,24},{1,5},{5... | collective-permute-start | bytes 393224 | tf_op jit(solution)/shard_map/ppermute | solution.py:26
  29.8 0.0 collective-permute-done.3.refs_1_
  29.9 0.3 partial.1.sum_ref
  30.2 0.0 collective-permute-done.9.refs_5_
  30.2 0.5 %collective-permute-done.8.refs_4_ = bf16[256,256]{1,0:T(8,128)(2,1)S(1)} collective-permute-done((bf16[256,256]{1,0:T(8,128)(2,1)S(1)}, bf16[256,256]{1,0:T(8,128)(2,1)S(1)}, u32[]{:S(2)}, u32[]{:S(2)}) %collective-permute-start.8) | collective-permute-done | bytes 131104 | tf_op jit(solution)/shard_map/ppermute | solution.py:26
  30.7 0.2 collective-permute-done.7.refs_3_
  30.9 0.0 copy-done.1
  30.9 1.3 %finish.1 = f32[2,2,128,256]{3,2,1,0:T(8,128)} custom-call(bf16[8,256,512]{2,1,0:T(8,128)(2,1)S(1)} %get-tuple-element.12.table_ref, f32[16,256]{1,0:T(8,128)S(1)} %copy-done.1, f32[256,512]{1,0:T(8,128)S(1)} %partial.1.sum_ref, bf16[256,256]{1,0:T(8,128)(2,1)S(1)} %collective-permute-done.4.refs_0_, bf16[256,256]{1,0:T(8,128)(2,1)S(1)} %collective-permute-done.5.refs_1_, ...), custom_call_target="tpu_custom_call" | custom-call | tf_op jit(solution)/shard_map/finish/pallas_call | solution.py:283
  (5 shorter events, 0.0 us)
Async XLA Ops:
  0.0 1.0 %copy-start = (bf16[128,2,2,512]{3,2,1,0:T(2,128)(2,1)S(1)}, bf16[128,2,2,512]{3,2,1,0:T(2,128)(2,1)}, u32[]{:S(2)}) copy-start(bf16[128,2,2,512]{3,2,1,0:T(2,128)(2,1)} %x_ref.1) | copy-start | bytes 1572868
  1.0 0.7 %copy-start.2 = (s32[3,2]{0,1:T(2,128)S(1)}, s32[3,2]{0,1:T(2,128)}, u32[]{:S(2)}) copy-start(s32[3,2]{0,1:T(2,128)} %param.8) | copy-start | bytes 76
  1.7 0.7 %copy-start.3 = (s32[3,2]{0,1:T(2,128)S(1)}, s32[3,2]{0,1:T(2,128)}, u32[]{:S(2)}) copy-start(s32[3,2]{0,1:T(2,128)} %param.10) | copy-start | bytes 76
  2.4 28.5 %copy-start.1 = (f32[16,256]{1,0:T(8,128)S(1)}, f32[16,256]{1,0:T(8,128)}, u32[]{:S(2)}) copy-start(f32[16,256]{1,0:T(8,128)} %energy_ref.1) | copy-start | bytes 49156
  3.1 9.7 %collective-permute-start = (bf16[132,2,2,128]{3,2,1,0:T(2,128)(2,1)S(1)}, bf16[132,2,2,128]{3,2,1,0:T(2,128)(2,1)S(1)}, u32[]{:S(2)}, u32[]{:S(2)}) collective-permute-start(bf16[132,2,2,128]{3,2,1,0:T(2,128)(2,1)S(1)} %get-tuple-element.15), channel_id=1, source_target_pairs={{0,3},{1,2},{2,1},{3,0},{4,7},{5,6},{6,5},{7,4},{8,11},{9,10},{10,... | collective-permute-start | bytes 405512 | tf_op jit(solution)/shard_map/ppermute | solution.py:26
  8.2 11.4 %collective-permute-start.1 = (bf16[132,2,2,128]{3,2,1,0:T(2,128)(2,1)S(1)}, bf16[132,2,2,128]{3,2,1,0:T(2,128)(2,1)S(1)}, u32[]{:S(2)}, u32[]{:S(2)}) collective-permute-start(bf16[132,2,2,128]{3,2,1,0:T(2,128)(2,1)S(1)} %get-tuple-element.16), channel_id=1, source_target_pairs={{0,2},{1,3},{2,0},{3,1},{4,6},{5,7},{6,4},{7,5},{8,10},{9,11},{10,... | collective-permute-start | bytes 405512 | tf_op jit(solution)/shard_map/ppermute | solution.py:26
  8.2 11.4 %collective-permute-start.2 = (bf16[132,2,2,128]{3,2,1,0:T(2,128)(2,1)S(1)}, bf16[132,2,2,128]{3,2,1,0:T(2,128)(2,1)S(1)}, u32[]{:S(2)}, u32[]{:S(2)}) collective-permute-start(bf16[132,2,2,128]{3,2,1,0:T(2,128)(2,1)S(1)} %get-tuple-element.17), channel_id=1, source_target_pairs={{0,1},{1,0},{2,3},{3,2},{4,5},{5,4},{6,7},{7,6},{8,9},{9,8},{10,11... | collective-permute-start | bytes 405512 | tf_op jit(solution)/shard_map/ppermute | solution.py:26
  8.8 0.7 %copy-start.4 = (s32[3,1024]{1,0:T(4,128)S(1)}, s32[3,1024]{1,0:T(4,128)}, u32[]{:S(2)}) copy-start(s32[3,1024]{1,0:T(4,128)} %rp_ref.1) | copy-start | bytes 36868
  9.6 0.7 %copy-start.5 = (s32[3,256]{1,0:T(4,128)S(1)}, s32[3,256]{1,0:T(4,128)}, u32[]{:S(2)}) copy-start(s32[3,256]{1,0:T(4,128)} %q_ref.1) | copy-start | bytes 9220
  20.0 5.8 %collective-permute-start.6 = (bf16[256,256]{1,0:T(8,128)(2,1)S(1)}, bf16[256,256]{1,0:T(8,128)(2,1)S(1)}, u32[]{:S(2)}, u32[]{:S(2)}) collective-permute-start(bf16[256,256]{1,0:T(8,128)(2,1)S(1)} %combine.1.refs_0_), channel_id=1, source_target_pairs={{0,8},{4,12},{8,0},{12,4},{16,24},{20,28},{24,16},{28,20},{1,9},{5... | collective-permute-start | bytes 393224 | tf_op jit(solution)/shard_map/ppermute | solution.py:26
  21.6 7.8 %collective-permute-start.5 = (bf16[256,256]{1,0:T(8,128)(2,1)S(1)}, bf16[256,256]{1,0:T(8,128)(2,1)S(1)}, u32[]{:S(2)}, u32[]{:S(2)}) collective-permute-start(bf16[256,256]{1,0:T(8,128)(2,1)S(1)} %combine.1.refs_0_), channel_id=1, source_target_pairs={{0,16},{4,20},{8,24},{12,28},{16,0},{20,4},{24,8},{28,12},{1,17},{... | collective-permute-start | bytes 393224 | tf_op jit(solution)/shard_map/ppermute | solution.py:26
  23.1 6.3 %collective-permute-start.4 = (bf16[256,256]{1,0:T(8,128)(2,1)S(1)}, bf16[256,256]{1,0:T(8,128)(2,1)S(1)}, u32[]{:S(2)}, u32[]{:S(2)}) collective-permute-start(bf16[256,256]{1,0:T(8,128)(2,1)S(1)} %combine.1.refs_0_), channel_id=1, source_target_pairs={{0,24},{4,28},{8,16},{12,20},{16,8},{20,12},{24,0},{28,4},{1,25},{... | collective-permute-start | bytes 393224 | tf_op jit(solution)/shard_map/ppermute | solution.py:26
  23.6 6.3 %collective-permute-start.3 = (bf16[256,256]{1,0:T(8,128)(2,1)S(1)}, bf16[256,256]{1,0:T(8,128)(2,1)S(1)}, u32[]{:S(2)}, u32[]{:S(2)}) collective-permute-start(bf16[256,256]{1,0:T(8,128)(2,1)S(1)} %combine.1.refs_0_), channel_id=1, source_target_pairs={{0,4},{4,0},{8,12},{12,8},{16,20},{20,16},{24,28},{28,24},{1,5},{5... | collective-permute-start | bytes 393224 | tf_op jit(solution)/shard_map/ppermute | solution.py:26
  25.8 4.3 %collective-permute-start.9 = (bf16[256,256]{1,0:T(8,128)(2,1)S(1)}, bf16[256,256]{1,0:T(8,128)(2,1)S(1)}, u32[]{:S(2)}, u32[]{:S(2)}) collective-permute-start(bf16[256,256]{1,0:T(8,128)(2,1)S(1)} %collective-permute-done.6.refs_2_), channel_id=1, source_target_pairs={{0,4},{4,0},{8,12},{12,8},{16,20},{20,16},{24,28},{28,24},{1,5},{5... | collective-permute-start | bytes 393224 | tf_op jit(solution)/shard_map/ppermute | solution.py:26
  29.3 1.3 %collective-permute-start.8 = (bf16[256,256]{1,0:T(8,128)(2,1)S(1)}, bf16[256,256]{1,0:T(8,128)(2,1)S(1)}, u32[]{:S(2)}, u32[]{:S(2)}) collective-permute-start(bf16[256,256]{1,0:T(8,128)(2,1)S(1)} %collective-permute-done.5.refs_1_), channel_id=1, source_target_pairs={{0,4},{4,0},{8,12},{12,8},{16,20},{20,16},{24,28},{28,24},{1,5},{5... | collective-permute-start | bytes 393224 | tf_op jit(solution)/shard_map/ppermute | solution.py:26
  29.3 1.5 %collective-permute-start.7 = (bf16[256,256]{1,0:T(8,128)(2,1)S(1)}, bf16[256,256]{1,0:T(8,128)(2,1)S(1)}, u32[]{:S(2)}, u32[]{:S(2)}) collective-permute-start(bf16[256,256]{1,0:T(8,128)(2,1)S(1)} %collective-permute-done.4.refs_0_), channel_id=1, source_target_pairs={{0,4},{4,0},{8,12},{12,8},{16,20},{20,16},{24,28},{28,24},{1,5},{5... | collective-permute-start | bytes 393224 | tf_op jit(solution)/shard_map/ppermute | solution.py:26

commit v3 on v2

--- a/solution.py
+++ b/solution.py
@@ -15,11 +15,33 @@
 LANES = 128
 TAIL = 4
 SHARES = (1,)
-LATE = 2
+GROUPS = (0, 0, 1, 2, 0, 1, 1, 2)
+ROUNDS = "x123"
 
 
 def xor_pairs(count, step):
     return [(i, i ^ step) for i in range(count)]
+
+
+def rounds(count):
+    xor = {i: xor_pairs(count, i) for i in range(1, count)}
+    up = [(i, i + 1) for i in range(count - 1)]
+    down = [(j, i) for i, j in up]
+    middle = [(1, 2), (2, 1)]
+    ends = [(0, 3), (3, 0)]
+    return {
+        "x123": (xor[1], xor[2], xor[3]),
+        "x213": (xor[2], xor[1], xor[3]),
+        "ud23": (up, down, xor[2], xor[3]),
+        "ud32": (up, down, xor[3], xor[2]),
+        "u2d3": (up, xor[2], down, xor[3]),
+        "m213": (middle, xor[2], xor[1], ends),
+        "m231": (middle, xor[2], ends, xor[1]),
+        "m123": (middle, xor[1], xor[2], ends),
+        "2ud3": (xor[2], up, down, ends),
+        "2m13": (xor[2], middle, xor[1], ends),
+        "2m31": (xor[2], middle, ends, xor[1]),
+    }[ROUNDS]
 
 
 def swap(value, axis, count, step):
@@ -41,7 +63,8 @@
     for c, (first, rows) in enumerate(starts):
         for j, step in enumerate(steps):
             i = c * len(steps) + j
-            column = pl.multiple_of((me ^ step) * entries, LANES)
+            target = sum(jnp.where(me == one, two, 0) for one, two in step)
+            column = pl.multiple_of(target * entries, LANES)
             copies.append(
                 pltpu.make_async_copy(
                     x_ref.at[pl.ds(first, rows), :, :, pl.ds(column, entries)],
@@ -73,6 +96,10 @@
         copy.wait()
 
 
+def stay(array):
+    return pltpu.with_memory_space_constraint(array, pltpu.HBM)
+
+
 def cut(coupling, re_cells, k_points, starts, steps, entries):
     cells = coupling.shape[1]
     shapes = []
@@ -84,7 +111,7 @@
     return pl.pallas_call(
         functools.partial(cut_kernel, starts, steps, entries),
         out_shape=shapes,
-        in_specs=[pl.BlockSpec(memory_space=pl.ANY)] * 3,
+        in_specs=[pl.BlockSpec(memory_space=pltpu.HBM)] * 3,
         out_specs=[pl.BlockSpec(memory_space=pltpu.VMEM)] * len(shapes),
         scratch_shapes=[
             pltpu.SMEM(re_cells.shape[::-1], jnp.int32),
@@ -92,9 +119,9 @@
             pltpu.SemaphoreType.DMA((len(shapes),)),
             pltpu.SemaphoreType.DMA((2,)),
         ],
-        compiler_params=grant(4),
+        compiler_params=grant(2),
         name="cut",
-    )(coupling, re_cells.T, k_points.T)
+    )(*[stay(x) for x in (coupling, re_cells.T, k_points.T)])
 
 
 def circle(modulus):
@@ -216,9 +243,10 @@
     )(rp_cells, q_points)
 
 
-def partial_kernel(pieces, table_ref, *refs):
+def partial_kernel(pieces, more, table_ref, *refs):
     ins, out = refs[:-1], refs[-1]
     me = lax.axis_index("blk")
+    total = ins[-1][...] if more else None
     for i, (step, row, rows) in enumerate(pieces):
         part = lax.dot_general(
             ins[i][...],
@@ -226,19 +254,20 @@
             (((0,), (0,)), ((), ())),
             preferred_element_type=jnp.float32,
         )
-        if i == 0:
-            out[...] = part
-        else:
-            out[...] += part
-
-
-def partial(tables, blocks, pieces):
+        total = part if total is None else total + part
+    out[...] = total
+
+
+def partial(tables, held, total):
+    blocks = [value for value, _ in held]
+    pieces = [piece for _, piece in held]
     shape = (blocks[0].shape[1], tables.shape[2])
     depth = sum(piece[2] for piece in pieces)
+    more = [] if total is None else [total]
     return pl.pallas_call(
-        functools.partial(partial_kernel, pieces),
+        functools.partial(partial_kernel, pieces, bool(more)),
         out_shape=jax.ShapeDtypeStruct(shape, jnp.float32),
-        in_specs=[pl.BlockSpec(memory_space=pltpu.VMEM)] * (1 + len(blocks)),
+        in_specs=[pl.BlockSpec(memory_space=pltpu.VMEM)] * (1 + len(blocks) + len(more)),
         out_specs=pl.BlockSpec(memory_space=pltpu.VMEM),
         compiler_params=grant(8),
         cost_estimate=pl.CostEstimate(
@@ -247,7 +276,7 @@
             transcendentals=0,
         ),
         name="partial",
-    )(tables, *blocks)
+    )(tables, *blocks, *more)
 
 
 def finish_kernel(pieces, waves, entries, table_ref, energy_ref, sum_ref, *refs):
@@ -303,18 +332,20 @@
     for share in SHARES:
         starts.append((sum(r for _, r in starts), share * unit))
 
-    steps = tuple(range(wide - 1, -1, -1))
+    steps = rounds(wide)
+    home = [(i, i) for i in range(wide)]
     cuts = cut(coupling, re_cells, k_points, starts, steps, entries)
+    kept = cut(coupling, re_cells, k_points, starts, (home,), entries)
     tables, *circles = table(rp_cells, q_points, starts, slab)
 
     moved = []
     for i, block in enumerate(cuts):
-        step = steps[i % len(steps)]
-        moved.append(swap(block, "wide", wide, step) if step else block)
-    early, late = [], []
+        c, step = divmod(i, len(steps))
+        moved.append(lax.ppermute(block, "wide", steps[step]))
+    groups = {}
     row = 0
     for c, (_, rows) in enumerate(starts):
-        group = moved[c * len(steps) : (c + 1) * len(steps)]
+        group = [kept[c]] + moved[c * len(steps) : (c + 1) * len(steps)]
         mine = combine(circles, group, rows, cells, entries, waves)
         held = {0: mine}
         for step in range(blk - 2, 0, -2):
@@ -322,16 +353,19 @@
         for step in list(held):
             held[step + 1] = swap(held[step], "blk", blk, 1)
         for step, value in held.items():
-            final = c == len(starts) - 1 and step >= LATE
-            (late if final else early).append((value, (step, row, 2 * rows)))
+            name = GROUPS[step] if c == len(starts) - 1 else 0
+            groups.setdefault((c, name), []).append((value, (step, row, 2 * rows)))
         row += 2 * rows
-    total = partial(tables, [v for v, _ in early], [p for _, p in early])
+    total = None
+    names = sorted(groups)
+    for c, name in names[:-1]:
+        total = partial(tables, groups[c, name], total)
     return finish(
         tables,
         mode_energy,
         total,
-        [v for v, _ in late],
-        [p for _, p in late],
+        [v for v, _ in groups[names[-1]]],
+        [p for _, p in groups[names[-1]]],
         waves,
         entries,
     )
@@ -385,6 +419,7 @@
             and blk > 1
             and total // wide == LANES
             and cells == 2
+            and wide == 4
             and waves == 2
             and slab % 128 == 0
             and q_points.shape[1] % LANES == 0

time: 32.5 us -> 28.5 us (0.88)
  waiting for transfers between devices: 14.9 us -> 12.2 us
  local copies, waits for them, and re-layouts: 3.8 us -> 1.41 us
  Pallas kernels: 3.56 us -> 5.12 us
  starting transfers between devices: 9.85 us -> 9.27 us
    ppermute x10 -> x7, waiting for transfers between devices: 14.9 us -> 4.94 us  [swap(): return lax.ppermute(value, axis, xor_pairs(count, step))]
    ppermute x0 -> x3, waiting for transfers between devices: none -> 7.3 us  [direct(): moved.append(lax.ppermute(block, 'wide', steps[step]))]
    ppermute x10 -> x7, starting transfers between devices: 9.85 us -> 3.56 us  [swap(): return lax.ppermute(value, axis, xor_pairs(count, step))]
    ppermute x0 -> x3, starting transfers between devices: none -> 5.71 us  [direct(): moved.append(lax.ppermute(block, 'wide', steps[step]))]
    unnamed x12 -> x6, local copies, waits for them, and re-layouts: 3.8 us -> 1.41 us
    pallas_call x1 -> x2, Pallas kernels: 0.65 us -> 2 us  [cut(): pl.pallas_call(functools.partial(cut_kernel, starts, steps, entries), out...]
    pallas_call x1 -> x2, Pallas kernels: 0.31 us -> 0.79 us  [partial(): pl.pallas_call(functools.partial(partial_kernel, pieces, bool(more)), out...]
  transfers between devices with their start and end apart: 10 -> 10, of which waited for: 6 -> 5; matrix products, arithmetic and copies ran while one was open for 0% -> 0% of each run, Pallas kernels for 4% -> 9%
where the time goes in v3:
time: 28.5 us; the launch traced here: 28.1 us
  waiting for transfers between devices  12.2 us (43%)
  starting transfers between devices  9.27 us (33%)
  Pallas kernels  5.12 us (18%)
  local copies, waits for them, and re-layouts  1.41 us (5%)
    ppermute x3, waiting for transfers between devices, direct(): moved.append(lax.ppermute(block, 'wide', steps[step]))  7.3 us
    ppermute x3, starting transfers between devices, direct(): moved.append(lax.ppermute(block, 'wide', steps[step]))  5.71 us
    ppermute x7, waiting for transfers between devices, swap(): return lax.ppermute(value, axis, xor_pairs(count, step))  4.94 us
    ppermute x7, starting transfers between devices, swap(): return lax.ppermute(value, axis, xor_pairs(count, step))  3.56 us
    pallas_call x2, Pallas kernels, cut(): pl.pallas_call(functools.partial(cut_kernel, starts, steps, entries), out...  2 us
    unnamed x6, local copies, waits for them, and re-layouts  1.41 us
    pallas_call x1, Pallas kernels, finish(): pl.pallas_call(functools.partial(finish_kernel, pieces, waves, entries),...  1.07 us
    pallas_call x1, Pallas kernels, table(): pl.pallas_call(functools.partial(table_kernel, starts, slab), out_shape=[...  0.9 us
  transfers between devices with their start and end apart: 10, of which 5 were waited for; matrix products, arithmetic and copies ran while one was open for 0% of the time, Pallas kernels for 9%

profile of v3, /device:TPU:0, one launch (start us, length us, event | category | flops | bytes accessed | tf_op | source)
XLA Modules:
  0.0 28.1 jit_solution(12389283314829400762)
XLA Ops:
  0.0 1.1 %cut.3 = (bf16[132,2,2,128]{3,2,1,0:T(2,128)(2,1)S(1)}, bf16[132,2,2,128]{3,2,1,0:T(2,128)(2,1)S(1)}, bf16[132,2,2,128]{3,2,1,0:T(2,128)(2,1)S(1)}) custom-call(bf16[128,2,2,512]{3,2,1,0:T(2,128)(2,1)} %x_ref.3, s32[2,3]{1,0:T(2,128)} %bitcast.10, s32[2,3]{1,0:T(2,128)} %bitcast.12), custom_call_target="tpu_custom_call" | custom-call | tf_op jit(solution)/shard_map/cut/pallas_call | solution.py:111
  1.1 3.1 %collective-permute-start = (bf16[132,2,2,128]{3,2,1,0:T(2,128)(2,1)S(1)}, bf16[132,2,2,128]{3,2,1,0:T(2,128)(2,1)S(1)}, u32[]{:S(2)}, u32[]{:S(2)}) collective-permute-start(bf16[132,2,2,128]{3,2,1,0:T(2,128)(2,1)S(1)} %get-tuple-element.14), channel_id=1, source_target_pairs={{0,1},{1,0},{2,3},{3,2},{4,5},{5,4},{6,7},{7,6},{8,9},{9,8},{10,11... | collective-permute-start | bytes 405512 | tf_op jit(solution)/shard_map/ppermute | solution.py:344
  4.2 2.6 %collective-permute-start.1 = (bf16[132,2,2,128]{3,2,1,0:T(2,128)(2,1)S(1)}, bf16[132,2,2,128]{3,2,1,0:T(2,128)(2,1)S(1)}, u32[]{:S(2)}, u32[]{:S(2)}) collective-permute-start(bf16[132,2,2,128]{3,2,1,0:T(2,128)(2,1)S(1)} %get-tuple-element.15), channel_id=1, source_target_pairs={{0,2},{1,3},{2,0},{3,1},{4,6},{5,7},{6,4},{7,5},{8,10},{9,11},{10,... | collective-permute-start | bytes 405512 | tf_op jit(solution)/shard_map/ppermute | solution.py:344
  6.8 0.0 collective-permute-start.2
  6.8 0.9 %cut.2 = bf16[132,2,2,128]{3,2,1,0:T(2,128)(2,1)S(1)} custom-call(bf16[128,2,2,512]{3,2,1,0:T(2,128)(2,1)} %x_ref.3, s32[2,3]{1,0:T(2,128)} %bitcast.11, s32[2,3]{1,0:T(2,128)} %bitcast.13), custom_call_target="tpu_custom_call" | custom-call | tf_op jit(solution)/shard_map/cut/pallas_call | solution.py:111
  7.7 0.0 copy-start.1
  7.7 0.7 %copy-done.1 = s32[3,1024]{1,0:T(4,128)S(1)} copy-done((s32[3,1024]{1,0:T(4,128)S(1)}, s32[3,1024]{1,0:T(4,128)}, u32[]{:S(2)}) %copy-start.1) | copy-done | bytes 12312
  8.5 0.7 %copy-done.2 = s32[3,256]{1,0:T(4,128)S(1)} copy-done((s32[3,256]{1,0:T(4,128)S(1)}, s32[3,256]{1,0:T(4,128)}, u32[]{:S(2)}) %copy-start.2) | copy-done | bytes 3096
  9.1 0.9 %table.1 = (bf16[8,256,512]{2,1,0:T(8,128)(2,1)S(1)}, f32[8,128]{1,0:T(8,128)S(1)}, f32[8,128]{1,0:T(8,128)S(1)}) custom-call(s32[3,1024]{1,0:T(4,128)S(1)} %copy-done.1, s32[3,256]{1,0:T(4,128)S(1)} %copy-done.2), custom_call_target="tpu_custom_call" | custom-call | flops 20971520 | bytes 2097152 | tf_op jit(solution)/shard_map/table/pallas_call | solution.py:227
  10.0 0.0 collective-permute-done
  10.1 7.3 %collective-permute-done.1 = bf16[132,2,2,128]{3,2,1,0:T(2,128)(2,1)S(1)} collective-permute-done((bf16[132,2,2,128]{3,2,1,0:T(2,128)(2,1)S(1)}, bf16[132,2,2,128]{3,2,1,0:T(2,128)(2,1)S(1)}, u32[]{:S(2)}, u32[]{:S(2)}) %collective-permute-start.1) | collective-permute-done | bytes 135200 | tf_op jit(solution)/shard_map/ppermute | solution.py:344
  17.4 0.0 collective-permute-done.2
  17.4 0.4 %combine.1.refs_0_ = bf16[256,256]{1,0:T(8,128)(2,1)S(1)} custom-call(f32[8,128]{1,0:T(8,128)S(1)} %get-tuple-element.12.cos_ref, f32[8,128]{1,0:T(8,128)S(1)} %get-tuple-element.13.sin_ref, bf16[528,128]{1,0:T(8,128)(2,1)S(1)} %bitcast.6, bf16[528,128]{1,0:T(8,128)(2,1)S(1)} %bitcast.7, bf16[528,128]{1,0:T(8,128)(2,1)S(1)} %bitcast.8, ...), custom_call_target="tpu_custom_call" | custom-call | tf_op jit(solution)/shard_map/combine/pallas_call | solution.py:173
  17.7 1.6 %collective-permute-start.5 = (bf16[256,256]{1,0:T(8,128)(2,1)S(1)}, bf16[256,256]{1,0:T(8,128)(2,1)S(1)}, u32[]{:S(2)}, u32[]{:S(2)}) collective-permute-start(bf16[256,256]{1,0:T(8,128)(2,1)S(1)} %combine.1.refs_0_), channel_id=1, source_target_pairs={{0,16},{4,20},{8,24},{12,28},{16,0},{20,4},{24,8},{28,12},{1,17},{... | collective-permute-start | bytes 393224 | tf_op jit(solution)/shard_map/ppermute | solution.py:48
  19.3 1.4 %collective-permute-start.3 = (bf16[256,256]{1,0:T(8,128)(2,1)S(1)}, bf16[256,256]{1,0:T(8,128)(2,1)S(1)}, u32[]{:S(2)}, u32[]{:S(2)}) collective-permute-start(bf16[256,256]{1,0:T(8,128)(2,1)S(1)} %combine.1.refs_0_), channel_id=1, source_target_pairs={{0,24},{4,28},{8,16},{12,20},{16,8},{20,12},{24,0},{28,4},{1,25},{... | collective-permute-start | bytes 393224 | tf_op jit(solution)/shard_map/ppermute | solution.py:48
  20.7 0.5 %collective-permute-start.4 = (bf16[256,256]{1,0:T(8,128)(2,1)S(1)}, bf16[256,256]{1,0:T(8,128)(2,1)S(1)}, u32[]{:S(2)}, u32[]{:S(2)}) collective-permute-start(bf16[256,256]{1,0:T(8,128)(2,1)S(1)} %combine.1.refs_0_), channel_id=1, source_target_pairs={{0,8},{4,12},{8,0},{12,4},{16,24},{20,28},{24,16},{28,20},{1,9},{5... | collective-permute-start | bytes 393224 | tf_op jit(solution)/shard_map/ppermute | solution.py:48
  21.3 0.0 collective-permute-start.7
  21.3 1.5 %collective-permute-done.5.refs_1_ = bf16[256,256]{1,0:T(8,128)(2,1)S(1)} collective-permute-done((bf16[256,256]{1,0:T(8,128)(2,1)S(1)}, bf16[256,256]{1,0:T(8,128)(2,1)S(1)}, u32[]{:S(2)}, u32[]{:S(2)}) %collective-permute-start.5) | collective-permute-done | bytes 131104 | tf_op jit(solution)/shard_map/ppermute | solution.py:48
  22.8 0.0 collective-permute-start.6
  22.8 2.4 %collective-permute-done.3.refs_0_ = bf16[256,256]{1,0:T(8,128)(2,1)S(1)} collective-permute-done((bf16[256,256]{1,0:T(8,128)(2,1)S(1)}, bf16[256,256]{1,0:T(8,128)(2,1)S(1)}, u32[]{:S(2)}, u32[]{:S(2)}) %collective-permute-start.3) | collective-permute-done | bytes 131104 | tf_op jit(solution)/shard_map/ppermute | solution.py:48
  25.2 0.0 collective-permute-start.8
  25.2 0.5 %collective-permute-done.4.refs_1_ = bf16[256,256]{1,0:T(8,128)(2,1)S(1)} collective-permute-done((bf16[256,256]{1,0:T(8,128)(2,1)S(1)}, bf16[256,256]{1,0:T(8,128)(2,1)S(1)}, u32[]{:S(2)}, u32[]{:S(2)}) %collective-permute-start.4) | collective-permute-done | bytes 131104 | tf_op jit(solution)/shard_map/ppermute | solution.py:48
  25.7 0.0 collective-permute-start.9
  25.7 0.0 collective-permute-done.7.refs_2_
  25.7 0.4 %partial.2.refs_3_ = f32[256,512]{1,0:T(8,128)S(1)} custom-call(bf16[8,256,512]{2,1,0:T(8,128)(2,1)S(1)} %get-tuple-element.11.table_ref, bf16[256,256]{1,0:T(8,128)(2,1)S(1)} %combine.1.refs_0_, bf16[256,256]{1,0:T(8,128)(2,1)S(1)} %collective-permute-done.5.refs_1_, bf16[256,256]{1,0:T(8,128)(2,1)S(1)} %collective-permute-done.7.refs_2_), custom_call_target="tpu_custom_call" | custom-call | flops 201326592 | bytes 524288 | tf_op jit(solution)/shard_map/partial/pallas_call | solution.py:267
  26.1 0.0 copy-start
  26.1 0.0 collective-permute-done.6.refs_2_
  26.1 0.4 %partial.3.sum_ref = f32[256,512]{1,0:T(8,128)S(1)} custom-call(bf16[8,256,512]{2,1,0:T(8,128)(2,1)S(1)} %get-tuple-element.11.table_ref, bf16[256,256]{1,0:T(8,128)(2,1)S(1)} %collective-permute-done.3.refs_0_, bf16[256,256]{1,0:T(8,128)(2,1)S(1)} %collective-permute-done.4.refs_1_, bf16[256,256]{1,0:T(8,128)(2,1)S(1)} %collective-permute-done.6.refs_2_, ...), custom_call_target="tpu_custom_call" | custom-call | flops 201326592 | bytes 524288 | tf_op jit(solution)/shard_map/partial/pallas_call | solution.py:267
  26.5 0.0 collective-permute-done.8.refs_0_
  26.6 0.5 %collective-permute-done.9.refs_1_ = bf16[256,256]{1,0:T(8,128)(2,1)S(1)} collective-permute-done((bf16[256,256]{1,0:T(8,128)(2,1)S(1)}, bf16[256,256]{1,0:T(8,128)(2,1)S(1)}, u32[]{:S(2)}, u32[]{:S(2)}) %collective-permute-start.9) | collective-permute-done | bytes 131104 | tf_op jit(solution)/shard_map/ppermute | solution.py:48
  27.1 0.0 copy-done
  27.1 1.1 %finish.1 = f32[2,2,128,256]{3,2,1,0:T(8,128)} custom-call(bf16[8,256,512]{2,1,0:T(8,128)(2,1)S(1)} %get-tuple-element.11.table_ref, f32[16,256]{1,0:T(8,128)S(1)} %copy-done, f32[256,512]{1,0:T(8,128)S(1)} %partial.3.sum_ref, bf16[256,256]{1,0:T(8,128)(2,1)S(1)} %collective-permute-done.8.refs_0_, bf16[256,256]{1,0:T(8,128)(2,1)S(1)} %collective-permute-done.9.refs_1_), custom_call_target="tpu_custom_call" | custom-call | tf_op jit(solution)/shard_map/finish/pallas_call | solution.py:312
  (1 shorter events, 0.0 us)
Async XLA Ops:
  1.1 9.0 %collective-permute-start = (bf16[132,2,2,128]{3,2,1,0:T(2,128)(2,1)S(1)}, bf16[132,2,2,128]{3,2,1,0:T(2,128)(2,1)S(1)}, u32[]{:S(2)}, u32[]{:S(2)}) collective-permute-start(bf16[132,2,2,128]{3,2,1,0:T(2,128)(2,1)S(1)} %get-tuple-element.14), channel_id=1, source_target_pairs={{0,1},{1,0},{2,3},{3,2},{4,5},{5,4},{6,7},{7,6},{8,9},{9,8},{10,11... | collective-permute-start | bytes 405512 | tf_op jit(solution)/shard_map/ppermute | solution.py:344
  4.2 13.2 %collective-permute-start.1 = (bf16[132,2,2,128]{3,2,1,0:T(2,128)(2,1)S(1)}, bf16[132,2,2,128]{3,2,1,0:T(2,128)(2,1)S(1)}, u32[]{:S(2)}, u32[]{:S(2)}) collective-permute-start(bf16[132,2,2,128]{3,2,1,0:T(2,128)(2,1)S(1)} %get-tuple-element.15), channel_id=1, source_target_pairs={{0,2},{1,3},{2,0},{3,1},{4,6},{5,7},{6,4},{7,5},{8,10},{9,11},{10,... | collective-permute-start | bytes 405512 | tf_op jit(solution)/shard_map/ppermute | solution.py:344
  6.8 10.6 %collective-permute-start.2 = (bf16[132,2,2,128]{3,2,1,0:T(2,128)(2,1)S(1)}, bf16[132,2,2,128]{3,2,1,0:T(2,128)(2,1)S(1)}, u32[]{:S(2)}, u32[]{:S(2)}) collective-permute-start(bf16[132,2,2,128]{3,2,1,0:T(2,128)(2,1)S(1)} %get-tuple-element.16), channel_id=1, source_target_pairs={{0,3},{1,2},{2,1},{3,0},{4,7},{5,6},{6,5},{7,4},{8,11},{9,10},{10,... | collective-permute-start | bytes 405512 | tf_op jit(solution)/shard_map/ppermute | solution.py:344
  7.7 0.7 %copy-start.1 = (s32[3,1024]{1,0:T(4,128)S(1)}, s32[3,1024]{1,0:T(4,128)}, u32[]{:S(2)}) copy-start(s32[3,1024]{1,0:T(4,128)} %rp_ref.1) | copy-start | bytes 36868
  8.5 0.7 %copy-start.2 = (s32[3,256]{1,0:T(4,128)S(1)}, s32[3,256]{1,0:T(4,128)}, u32[]{:S(2)}) copy-start(s32[3,256]{1,0:T(4,128)} %q_ref.1) | copy-start | bytes 9220
  17.7 5.0 %collective-permute-start.5 = (bf16[256,256]{1,0:T(8,128)(2,1)S(1)}, bf16[256,256]{1,0:T(8,128)(2,1)S(1)}, u32[]{:S(2)}, u32[]{:S(2)}) collective-permute-start(bf16[256,256]{1,0:T(8,128)(2,1)S(1)} %combine.1.refs_0_), channel_id=1, source_target_pairs={{0,16},{4,20},{8,24},{12,28},{16,0},{20,4},{24,8},{28,12},{1,17},{... | collective-permute-start | bytes 393224 | tf_op jit(solution)/shard_map/ppermute | solution.py:48
  19.3 5.9 %collective-permute-start.3 = (bf16[256,256]{1,0:T(8,128)(2,1)S(1)}, bf16[256,256]{1,0:T(8,128)(2,1)S(1)}, u32[]{:S(2)}, u32[]{:S(2)}) collective-permute-start(bf16[256,256]{1,0:T(8,128)(2,1)S(1)} %combine.1.refs_0_), channel_id=1, source_target_pairs={{0,24},{4,28},{8,16},{12,20},{16,8},{20,12},{24,0},{28,4},{1,25},{... | collective-permute-start | bytes 393224 | tf_op jit(solution)/shard_map/ppermute | solution.py:48
  20.7 5.0 %collective-permute-start.4 = (bf16[256,256]{1,0:T(8,128)(2,1)S(1)}, bf16[256,256]{1,0:T(8,128)(2,1)S(1)}, u32[]{:S(2)}, u32[]{:S(2)}) collective-permute-start(bf16[256,256]{1,0:T(8,128)(2,1)S(1)} %combine.1.refs_0_), channel_id=1, source_target_pairs={{0,8},{4,12},{8,0},{12,4},{16,24},{20,28},{24,16},{28,20},{1,9},{5... | collective-permute-start | bytes 393224 | tf_op jit(solution)/shard_map/ppermute | solution.py:48
  21.3 4.4 %collective-permute-start.7 = (bf16[256,256]{1,0:T(8,128)(2,1)S(1)}, bf16[256,256]{1,0:T(8,128)(2,1)S(1)}, u32[]{:S(2)}, u32[]{:S(2)}) collective-permute-start(bf16[256,256]{1,0:T(8,128)(2,1)S(1)} %combine.1.refs_0_), channel_id=1, source_target_pairs={{0,4},{4,0},{8,12},{12,8},{16,20},{20,16},{24,28},{28,24},{1,5},{5... | collective-permute-start | bytes 393224 | tf_op jit(solution)/shard_map/ppermute | solution.py:48
  22.8 3.4 %collective-permute-start.6 = (bf16[256,256]{1,0:T(8,128)(2,1)S(1)}, bf16[256,256]{1,0:T(8,128)(2,1)S(1)}, u32[]{:S(2)}, u32[]{:S(2)}) collective-permute-start(bf16[256,256]{1,0:T(8,128)(2,1)S(1)} %collective-permute-done.5.refs_1_), channel_id=1, source_target_pairs={{0,4},{4,0},{8,12},{12,8},{16,20},{20,16},{24,28},{28,24},{1,5},{5... | collective-permute-start | bytes 393224 | tf_op jit(solution)/shard_map/ppermute | solution.py:48
  25.2 1.4 %collective-permute-start.8 = (bf16[256,256]{1,0:T(8,128)(2,1)S(1)}, bf16[256,256]{1,0:T(8,128)(2,1)S(1)}, u32[]{:S(2)}, u32[]{:S(2)}) collective-permute-start(bf16[256,256]{1,0:T(8,128)(2,1)S(1)} %collective-permute-done.3.refs_0_), channel_id=1, source_target_pairs={{0,4},{4,0},{8,12},{12,8},{16,20},{20,16},{24,28},{28,24},{1,5},{5... | collective-permute-start | bytes 393224 | tf_op jit(solution)/shard_map/ppermute | solution.py:48
  25.7 1.3 %collective-permute-start.9 = (bf16[256,256]{1,0:T(8,128)(2,1)S(1)}, bf16[256,256]{1,0:T(8,128)(2,1)S(1)}, u32[]{:S(2)}, u32[]{:S(2)}) collective-permute-start(bf16[256,256]{1,0:T(8,128)(2,1)S(1)} %collective-permute-done.4.refs_1_), channel_id=1, source_target_pairs={{0,4},{4,0},{8,12},{12,8},{16,20},{20,16},{24,28},{28,24},{1,5},{5... | collective-permute-start | bytes 393224 | tf_op jit(solution)/shard_map/ppermute | solution.py:48
  26.1 0.9 %copy-start = (f32[16,256]{1,0:T(8,128)S(1)}, f32[16,256]{1,0:T(8,128)}, u32[]{:S(2)}) copy-start(f32[16,256]{1,0:T(8,128)} %energy_ref.1) | copy-start | bytes 49156

commit v4 on v3

v4 whole, which is shorter than its diff:
```python
import functools
import math

import jax
import jax.numpy as jnp
from jax import lax
from jax.experimental import pallas as pl
from jax.experimental.pallas import tpu as pltpu
from jax.sharding import PartitionSpec as P


MODES = 16
MESHQ = 32
MESHK = 32
LANES = 128
TAIL = 4
NEAR = (4, 6, 2)
LAST = 96
ORDER = ("pair", "two", "three", "one", "sum")
EARLY = 1
CODED = 1
BITS = 14.0


def xor_pairs(count, step):
    return [(i, i ^ step) for i in range(count)]


def swap(value, axis, count, step):
    return lax.ppermute(value, axis, xor_pairs(count, step))


def grant(mebibytes):
    return pltpu.CompilerParams(vmem_limit_bytes=int(mebibytes * 2**20))


def cut_kernel(parts, rings, more, entries, x_ref, cells_ref, points_ref, *rest):
    extra, rest = rest[:more], rest[more:]
    outs = rest[: len(parts)]
    cells, points, sem, small = rest[-4:]
    me = lax.axis_index("wide")
    copies = [
        pltpu.make_async_copy(cells_ref, cells, small.at[0]),
        pltpu.make_async_copy(points_ref, points, small.at[1]),
    ]
    for i, (step, first, rows) in enumerate(parts):
        column = pl.multiple_of((me ^ step) * entries, LANES)
        copies.append(
            pltpu.make_async_copy(
                x_ref.at[pl.ds(first, rows), :, :, pl.ds(column, entries)],
                outs[i].at[pl.ds(0, rows)],
                sem.at[i],
            )
        )
    for i in range(more):
        out = rest[len(parts) + 2 * rings + i]
        copies.append(pltpu.make_async_copy(extra[i], out, small.at[2 + i]))
    for copy in copies:
        copy.start()
    if rings:
        rest[len(parts)][...], rest[len(parts) + 1][...] = circle(MESHK)
    for copy in copies[:2]:
        copy.wait()
    shape = (TAIL,) + outs[0].shape[1:]
    which_cell = lax.broadcasted_iota(jnp.int32, shape, 1)
    which_wave = lax.broadcasted_iota(jnp.int32, shape, 2)
    tail = jnp.zeros(shape, jnp.float32)
    for r in range(cells.shape[0]):
        for k in range(points.shape[0]):
            turn = cells[r, 0] * points[k, 0]
            for axis in range(1, cells.shape[1]):
                turn += cells[r, axis] * points[k, axis]
            turn = lax.rem(lax.rem(turn, MESHK) + MESHK, MESHK)
            here = (which_cell == r) & (which_wave == k)
            tail = jnp.where(here, turn.astype(jnp.float32), tail)
    tail = tail.astype(outs[0].dtype)
    for (_, _, rows), out in zip(parts, outs):
        out[pl.ds(rows, TAIL)] = tail
    for copy in copies[2:]:
        copy.wait()


def stay(array):
    return pltpu.with_memory_space_constraint(array, pltpu.HBM)


def cut(coupling, re_cells, k_points, parts, rings, extra, entries):
    cells = coupling.shape[1]
    shapes = [
        jax.ShapeDtypeStruct((rows + TAIL, cells, 2, entries), coupling.dtype)
        for _, _, rows in parts
    ]
    count = len(shapes)
    shapes += [jax.ShapeDtypeStruct((8, LANES), jnp.float32)] * (2 * rings)
    shapes += [jax.ShapeDtypeStruct(array.shape, array.dtype) for array in extra]
    arrays = (coupling, re_cells.T, k_points.T) + tuple(extra)
    outs = pl.pallas_call(
        functools.partial(cut_kernel, parts, rings, len(extra), entries),
        out_shape=shapes,
        in_specs=[pl.BlockSpec(memory_space=pltpu.HBM)] * len(arrays),
        out_specs=[pl.BlockSpec(memory_space=pltpu.VMEM)] * len(shapes),
        scratch_shapes=[
            pltpu.SMEM(re_cells.shape[::-1], jnp.int32),
            pltpu.SMEM(k_points.shape[::-1], jnp.int32),
            pltpu.SemaphoreType.DMA((count,)),
            pltpu.SemaphoreType.DMA((2 + len(extra),)),
        ],
        compiler_params=grant(2),
        name="cut",
    )(*[stay(array) for array in arrays])
    return outs[:count], outs[count:]


def circle(modulus):
    lane = lax.broadcasted_iota(jnp.int32, (8, LANES), 1) % modulus
    angle = lane.astype(jnp.float32) * (2.0 * math.pi / modulus)
    return jnp.cos(angle), jnp.sin(angle)


def look(values, index):
    return jnp.take_along_axis(values, index, axis=1, mode="promise_in_bounds")


def combine_kernel(spans, rows, cells, waves, adds, cos_ref, sin_ref, *refs):
    count = len(spans)
    ins, plus = refs[:count], refs[count : count + len(adds)]
    out, work, sums = refs[-3:]
    entries = work.shape[2]
    coded = out.dtype == jnp.int16
    target = sums if coded else out
    per = 2 * cells
    phases = []
    for i, ref in enumerate(ins):
        work[i, pl.ds(0, ref.shape[0]), :] = ref[...].astype(jnp.float32)
    for i, (_, size) in enumerate(spans):
        turn = work[i, pl.ds(size * per, 8), :].astype(jnp.int32)
        phases.append((look(cos_ref[...], turn), look(sin_ref[...], turn)))
    step = 32
    for first in range(0, rows, step):
        re = [None] * waves
        im = [None] * waves
        for (begin, size), ref in zip(adds, plus):
            if not begin <= first < begin + size:
                continue
            for k in range(waves):
                lanes = pl.ds(k * entries, entries)
                x = ref[pl.ds(first - begin, step), lanes].astype(jnp.float32)
                y = ref[pl.ds(size + first - begin, step), lanes].astype(jnp.float32)
                if ref.dtype == jnp.int16:
                    power = ref[pl.ds(2 * size, 16), lanes].astype(jnp.float32)
                    unit = jnp.exp2(power[0:1, :] - BITS)
                    x, y = x * unit, y * unit
                re[k] = x if re[k] is None else re[k] + x
                im[k] = y if im[k] is None else im[k] + y
        for i, (begin, size) in enumerate(spans):
            if not begin <= first < begin + size:
                continue
            cos, sin = phases[i]
            for r in range(cells):
                start = (first - begin) * per + 2 * r
                a = work[i, pl.ds(start, step, stride=per), :]
                b = work[i, pl.ds(start + 1, step, stride=per), :]
                for k in range(waves):
                    at = r * waves + k
                    c = cos[at : at + 1, :]
                    s = sin[at : at + 1, :]
                    x = c * a - s * b
                    y = c * b + s * a
                    re[k] = x if re[k] is None else re[k] + x
                    im[k] = y if im[k] is None else im[k] + y
        for k in range(waves):
            lanes = pl.ds(k * entries, entries)
            target[pl.ds(first, step), lanes] = re[k].astype(target.dtype)
            target[pl.ds(rows + first, step), lanes] = im[k].astype(target.dtype)
    if coded:
        value = sums[...]
        top = jnp.max(jnp.abs(value), axis=0, keepdims=True)
        power = jnp.ceil(jnp.log2(jnp.maximum(top, 2.0**-100)))
        scaled = jnp.round(value * jnp.exp2(BITS - power)).astype(jnp.int32)
        out[pl.ds(0, 2 * rows), :] = scaled.astype(jnp.int16)
        spread = jnp.broadcast_to(power, (16, value.shape[1])).astype(jnp.int32)
        out[pl.ds(2 * rows, 16), :] = spread.astype(jnp.int16)


def combine(circles, blocks, spans, plus, adds, rows, waves, dtype):
    cells, _, entries = blocks[0].shape[1:]
    flat = [b.reshape(b.shape[0] * 2 * cells, entries) for b in blocks]
    full = max(b.shape[0] for b in flat)
    coded = dtype == jnp.int16
    shape = (2 * rows, waves * entries)
    tall = (2 * rows + 16 * coded, waves * entries)
    return pl.pallas_call(
        functools.partial(combine_kernel, spans, rows, cells, waves, adds),
        out_shape=jax.ShapeDtypeStruct(tall, dtype),
        in_specs=[pl.BlockSpec(memory_space=pltpu.VMEM)] * (2 + len(flat) + len(plus)),
        out_specs=pl.BlockSpec(memory_space=pltpu.VMEM),
        scratch_shapes=[
            pltpu.VMEM((len(flat), full, entries), jnp.float32),
            pltpu.VMEM(shape if coded else (8, LANES), jnp.float32),
        ],
        compiler_params=grant(6),
        name="combine",
    )(*circles, *flat, *plus)


def table_kernel(slab, rp_ref, q_ref, out_ref):
    cos_table, sin_table = circle(MESHQ)
    blocks = out_ref.shape[0]
    q_local = q_ref.shape[1]
    step = 32
    q = q_ref[...].astype(jnp.bfloat16)
    for block in range(blocks):
        n = lax.dot_general(
            rp_ref[:, pl.ds(block * slab, slab)].astype(jnp.bfloat16),
            q,
            (((0,), (0,)), ((), ())),
            preferred_element_type=jnp.float32,
        )
        m = n - MESHQ * jnp.floor(n * (1.0 / MESHQ))
        index = m.astype(jnp.int32)
        for top in range(0, slab, step):
            for left in range(0, q_local, LANES):
                cos_rows = []
                sin_rows = []
                for sub in range(top, top + step, 8):
                    at = index[sub : sub + 8, left : left + LANES]
                    cos_rows.append(look(cos_table, at))
                    sin_rows.append(look(sin_table, at))
                c = jnp.concatenate(cos_rows, axis=0).astype(jnp.bfloat16)
                s = jnp.concatenate(sin_rows, axis=0).astype(jnp.bfloat16)
                near = pl.ds(left, LANES)
                far = pl.ds(q_local + left, LANES)
                out_ref[block, pl.ds(top, step), near] = c
                out_ref[block, pl.ds(top, step), far] = s
                out_ref[block, pl.ds(slab + top, step), near] = -s
                out_ref[block, pl.ds(slab + top, step), far] = c


def table(rp_cells, q_points, slab):
    blocks = rp_cells.shape[1] // slab
    q_local = q_points.shape[1]
    shape = (blocks, 2 * slab, 2 * q_local)
    return pl.pallas_call(
        functools.partial(table_kernel, slab),
        out_shape=jax.ShapeDtypeStruct(shape, jnp.bfloat16),
        in_specs=[pl.BlockSpec(memory_space=pltpu.VMEM)] * 2,
        out_specs=pl.BlockSpec(memory_space=pltpu.VMEM),
        compiler_params=grant(6),
        cost_estimate=pl.CostEstimate(
            flops=8 * blocks * slab * q_local * 10,
            bytes_accessed=blocks * slab * q_local * 8,
            transcendentals=0,
        ),
        name="table",
    )(rp_cells, q_points)


def partial_kernel(pieces, more, table_ref, *refs):
    ins, out = refs[:-1], refs[-1]
    me = lax.axis_index("blk")
    total = ins[-1][...] if more else None
    for i, step in enumerate(pieces):
        part = lax.dot_general(
            ins[i][...],
            table_ref[me ^ step],
            (((0,), (0,)), ((), ())),
            preferred_element_type=jnp.float32,
        )
        total = part if total is None else total + part
    out[...] = total


def partial(tables, held, total):
    blocks = [value for value, _ in held]
    pieces = [piece for _, piece in held]
    shape = (blocks[0].shape[1], tables.shape[2])
    depth = len(pieces) * tables.shape[1]
    more = [] if total is None else [total]
    return pl.pallas_call(
        functools.partial(partial_kernel, pieces, bool(more)),
        out_shape=jax.ShapeDtypeStruct(shape, jnp.float32),
        in_specs=[pl.BlockSpec(memory_space=pltpu.VMEM)] * (1 + len(blocks) + len(more)),
        out_specs=pl.BlockSpec(memory_space=pltpu.VMEM),
        compiler_params=grant(8),
        cost_estimate=pl.CostEstimate(
            flops=2 * depth * shape[0] * shape[1],
            bytes_accessed=4 * shape[0] * shape[1],
            transcendentals=0,
        ),
        name="partial",
    )(tables, *blocks, *more)


def finish_kernel(pieces, waves, entries, table_ref, energy_ref, sum_ref, *refs):
    ins, out, held, sem = refs[:-3], refs[-3], refs[-2], refs[-1]
    me = lax.axis_index("blk")
    q_local = energy_ref.shape[1]
    weight = 1.0 / jnp.sqrt(2.0 * energy_ref[...])
    copies = []
    for k in range(waves):
        lanes = pl.ds(k * entries, entries)
        total = sum_ref[lanes, :]
        for i, step in enumerate(pieces):
            total += lax.dot_general(
                ins[i][:, lanes],
                table_ref[me ^ step],
                (((0,), (0,)), ((), ())),
                preferred_element_type=jnp.float32,
            )
        for part in range(2):
            for e in range(0, entries, MODES):
                held[k, part, pl.ds(e, MODES), :] = (
                    total[e : e + MODES, part * q_local : (part + 1) * q_local] * weight
                )
        copies.append(pltpu.make_async_copy(held.at[k], out.at[k], sem.at[k]))
        copies[-1].start()
    for copy in copies:
        copy.wait()


def finish(tables, energy, total, blocks, pieces, waves, entries):
    q_local = energy.shape[1]
    shape = (waves, 2, entries, q_local)
    return pl.pallas_call(
        functools.partial(finish_kernel, pieces, waves, entries),
        out_shape=jax.ShapeDtypeStruct(shape, jnp.float32),
        in_specs=[pl.BlockSpec(memory_space=pltpu.VMEM)] * (3 + len(blocks)),
        out_specs=pl.BlockSpec(memory_space=pl.ANY),
        scratch_shapes=[
            pltpu.VMEM(shape, jnp.float32),
            pltpu.SemaphoreType.DMA((waves,)),
        ],
        compiler_params=grant(8),
        name="finish",
    )(tables, energy, total, *blocks)


def direct(blk, wide, coupling, rp_cells, re_cells, q_points, k_points, mode_energy):
    slab, _, _, total = coupling.shape
    entries = total // wide
    waves = k_points.shape[1]
    most = slab - LAST
    rest = (most, LAST)

    sent = {"one": (1, 0, slab), "two": (2, 0, most), "three": (3, 0, most)}
    if LAST:
        sent["pair"] = (3, most, LAST)
    if not most:
        del sent["two"], sent["three"]
    names = [name for name in ORDER if name in sent]
    parts = [sent[name] for name in names] + [(2, most, LAST)] * bool(LAST)
    arrays = (coupling, re_cells, k_points)
    cuts, circles = cut(*arrays, parts, True, [], entries)
    mid = list(cuts[len(names) :])
    extra = (rp_cells, q_points)
    (own,), extra = cut(*arrays, [(0, 0, slab)], False, extra, entries)
    tables = table(*extra, slab)

    got = {}
    for name, block in zip(names, cuts):
        got[name] = swap(block, "wide", wide, 1 if name == "pair" else sent[name][0])
    plus, adds = [], []
    if LAST:
        dtype = jnp.int16 if CODED else jnp.bfloat16
        both = combine(
            circles, mid + [got["pair"]], [(0, LAST)] * 2, [], [], LAST, waves, dtype
        )
        plus.append(swap(both, "wide", wide, 2))
        adds.append(rest)
    blocks, spans = [own, got["one"]], [(0, slab)] * 2
    if EARLY:
        some = combine(circles, blocks, spans, [], [], slab, waves, jnp.float32)
        plus.append(some)
        adds.append((0, slab))
        blocks, spans = [], []
    if most:
        blocks += [got["two"], got["three"]]
        spans += [(0, most)] * 2
    mine = combine(circles, blocks, spans, plus, adds, slab, waves, jnp.bfloat16)

    held = {0: mine}
    for step in range(blk - 2, 0, -2):
        held[step] = swap(mine, "blk", blk, step)
    for step in list(held):
        held[step + 1] = swap(held[step], "blk", blk, 1)
    first, second, third = NEAR
    groups = [
        (0, 1, first),
        (third, first + 1, second),
        (third + 1, second + 1),
    ]
    total = None
    for steps in groups[:-1]:
        total = partial(tables, [(held[step], step) for step in steps], total)
    return finish(
        tables,
        mode_energy,
        total,
        [held[step] for step in groups[-1]],
        groups[-1],
        waves,
        entries,
    )


def phase_parts(left, right, modulus):
    whole = jnp.sum(left[:, :, None] * right[:, None, :], axis=0)
    angle = jnp.mod(whole, modulus).astype(jnp.float32) * (2.0 * math.pi / modulus)
    return (jnp.cos(angle), jnp.sin(angle))


def general(coupling, rp_cells, re_cells, q_points, k_points, mode_energy):
    moved = lax.all_to_all(coupling, "wide", split_axis=3, concat_axis=1, tiled=True)
    cells = lax.all_gather(re_cells, "wide", axis=1, tiled=True)
    entries = moved.shape[3]
    offset = lax.axis_index("wide") * entries
    k_cos, k_sin = phase_parts(k_points, cells, MESHK)
    real = moved[:, :, 0].astype(jnp.float32)
    imag = moved[:, :, 1].astype(jnp.float32)
    high = lax.Precision.HIGHEST
    turn = functools.partial(jnp.einsum, "kr,pre->pke", precision=high)
    held = jnp.stack(
        [turn(k_cos, real) - turn(k_sin, imag), turn(k_cos, imag) + turn(k_sin, real)],
        axis=2,
    ).astype(coupling.dtype)
    full = lax.all_gather(held, "blk", axis=0, tiled=True)
    cosine, sine = phase_parts(q_points, rp_cells, MESHQ)
    dot = functools.partial(
        jnp.einsum, "qp,pkse->skeq", preferred_element_type=jnp.float32
    )
    with_cos = dot(cosine.astype(full.dtype), full)
    with_sin = dot(sine.astype(full.dtype), full)
    index = (offset + jnp.arange(entries, dtype=jnp.int32)) % MODES
    weight = (1.0 / jnp.sqrt(2.0 * mode_energy))[index]
    return jnp.stack(
        [(with_cos[0] - with_sin[1]) * weight, (with_cos[1] + with_sin[0]) * weight],
        axis=1,
    )


def solution(mesh):
    blk, wide = mesh.shape["blk"], mesh.shape["wide"]

    def on_device(coupling, rp_cells, re_cells, q_points, k_points, mode_energy):
        args = (coupling, rp_cells, re_cells, q_points, k_points, mode_energy)
        slab, cells, _, total = coupling.shape
        waves = k_points.shape[1]
        fits = (
            blk == 8
            and total // wide == LANES
            and cells == 2
            and wide == 4
            and waves == 2
            and slab % 128 == 0
            and q_points.shape[1] % LANES == 0
        )
        if not fits:
            return general(*args)
        return direct(blk, wide, *args)

    in_specs = (
        P("blk", "wide", None, None),
        P(),
        P(None, "wide"),
        P(None, "blk"),
        P(),
        P(None, "blk"),
    )
    out_specs = P(None, None, "wide", "blk")
    return jax.shard_map(
        on_device, mesh=mesh, in_specs=in_specs, out_specs=out_specs, check_vma=False
    )
```

time: 28.5 us -> 30.3 us (1.063)
  starting transfers between devices: 9.27 us -> 13.9 us
  waiting for transfers between devices: 12.2 us -> 10.4 us
  local copies, waits for them, and re-layouts: 1.41 us -> 0.28 us
    ppermute x7 -> x12, starting transfers between devices: 3.56 us -> 13.9 us  [swap(): return lax.ppermute(value, axis, xor_pairs(count, step))]
    ppermute x3 -> x0, waiting for transfers between devices: 7.3 us -> none  [direct(): moved.append(lax.ppermute(block, 'wide', steps[step]))]
    ppermute x3 -> x0, starting transfers between devices: 5.71 us -> none  [direct(): moved.append(lax.ppermute(block, 'wide', steps[step]))]
    ppermute x7 -> x12, waiting for transfers between devices: 4.94 us -> 10.4 us  [swap(): return lax.ppermute(value, axis, xor_pairs(count, step))]
    unnamed x6 -> x2, local copies, waits for them, and re-layouts: 1.41 us -> 0.28 us
    pallas_call x4 -> x6, Pallas kernels: 3.27 us -> 3.56 us  [the longest x2 2.1 us: cut(): pl.pallas_call(functools.partial(cut_kernel, parts, rings, len(extra), en...]
  transfers between devices with their start and end apart: 10 -> 12, of which waited for: 5 -> 5; matrix products, arithmetic and copies ran while one was open for 0% -> 0% of each run, Pallas kernels for 9% -> 10%
where the time goes in v4:
time: 30.3 us; the launch traced here: 30.1 us
  starting transfers between devices  13.9 us (46%)
  waiting for transfers between devices  10.4 us (34%)
  Pallas kernels  5.41 us (18%)
    ppermute x12, starting transfers between devices, swap(): return lax.ppermute(value, axis, xor_pairs(count, step))  13.9 us
    ppermute x12, waiting for transfers between devices, swap(): return lax.ppermute(value, axis, xor_pairs(count, step))  10.4 us
    pallas_call x2, Pallas kernels, cut(): pl.pallas_call(functools.partial(cut_kernel, parts, rings, len(extra), en...  2.1 us
    pallas_call x1, Pallas kernels, finish(): pl.pallas_call(functools.partial(finish_kernel, pieces, waves, entries),...  1.06 us
    pallas_call x1, Pallas kernels, table(): pl.pallas_call(functools.partial(table_kernel, slab), out_shape=jax.Shape...  0.91 us
    pallas_call x2, Pallas kernels, partial(): pl.pallas_call(functools.partial(partial_kernel, pieces, bool(more)), out...  0.79 us
  transfers between devices with their start and end apart: 12, of which 5 were waited for; matrix products, arithmetic and copies ran while one was open for 0% of the time, Pallas kernels for 10%

profile of v4, /device:TPU:0, one launch (start us, length us, event | category | flops | bytes accessed | tf_op | source)
XLA Modules:
  0.0 30.1 jit_solution(16707248823700735618)
XLA Ops:
  0.0 1.1 %cut.3 = (bf16[100,2,2,128]{3,2,1,0:T(2,128)(2,1)S(1)}, bf16[36,2,2,128]{3,2,1,0:T(2,128)(2,1)S(1)}, bf16[36,2,2,128]{3,2,1,0:T(2,128)(2,1)S(1)}, bf16[132,2,2,1...) custom-call(bf16[128,2,2,512]{3,2,1,0:T(2,128)(2,1)} %x_ref.3, ...), custom_call_target="tpu_custom_call" | custom-call | tf_op jit(solution)/shard_map/cut/pallas_call | solution.py:97
  1.1 3.1 %collective-permute-start.2 = (bf16[100,2,2,128]{3,2,1,0:T(2,128)(2,1)S(1)}, bf16[100,2,2,128]{3,2,1,0:T(2,128)(2,1)S(1)}, u32[]{:S(2)}, u32[]{:S(2)}) collective-permute-start(bf16[100,2,2,128]{3,2,1,0:T(2,128)(2,1)S(1)} %get-tuple-element.22), channel_id=1, source_target_pairs={{0,1},{1,0},{2,3},{3,2},{4,5},{5,4},{6,7},{7,6},{8,9},{9,8},{10,11... | collective-permute-start | bytes 307208 | tf_op jit(solution)/shard_map/ppermute | solution.py:30
  4.2 0.1 collective-permute-start.4
  4.3 3.5 %collective-permute-done.2 = bf16[100,2,2,128]{3,2,1,0:T(2,128)(2,1)S(1)} collective-permute-done((bf16[100,2,2,128]{3,2,1,0:T(2,128)(2,1)S(1)}, bf16[100,2,2,128]{3,2,1,0:T(2,128)(2,1)S(1)}, u32[]{:S(2)}, u32[]{:S(2)}) %collective-permute-start.2) | collective-permute-done | bytes 102432 | tf_op jit(solution)/shard_map/ppermute | solution.py:30
  7.9 0.2 combine.3
  8.1 3.1 %collective-permute-start.3 = (s16[208,256]{1,0:T(8,128)(2,1)S(1)}, s16[208,256]{1,0:T(8,128)(2,1)S(1)}, u32[]{:S(2)}, u32[]{:S(2)}) collective-permute-start(s16[208,256]{1,0:T(8,128)(2,1)S(1)} %combine.3), channel_id=1, source_target_pairs={{0,2},{1,3},{2,0},{3,1},{4,6},{5,7},{6,4},{7,5},{8,10},{9,11},{10,... | collective-permute-start | bytes 319496 | tf_op jit(solution)/shard_map/ppermute | solution.py:30
  11.1 0.1 collective-permute-start
  11.2 4.0 %collective-permute-start.1 = (bf16[36,2,2,128]{3,2,1,0:T(2,128)(2,1)S(1)}, bf16[36,2,2,128]{3,2,1,0:T(2,128)(2,1)S(1)}, u32[]{:S(2)}, u32[]{:S(2)}) collective-permute-start(bf16[36,2,2,128]{3,2,1,0:T(2,128)(2,1)S(1)} %get-tuple-element.20), channel_id=1, source_target_pairs={{0,3},{1,2},{2,1},{3,0},{4,7},{5,6},{6,5},{7,4},{8,11},{9,10},{10,... | collective-permute-start | bytes 110600 | tf_op jit(solution)/shard_map/ppermute | solution.py:30
  15.2 1.0 %cut.2 = (bf16[132,2,2,128]{3,2,1,0:T(2,128)(2,1)S(1)}, s32[3,1024]{1,0:T(4,128)S(1)}, s32[3,256]{1,0:T(4,128)S(1)}) custom-call(bf16[128,2,2,512]{3,2,1,0:T(2,128)(2,1)} %x_ref.3, s32[2,3]{1,0:T(2,128)} %bitcast.15, s32[2,3]{1,0:T(2,128)} %bitcast.17, s32[3,1024]{1,0:T(4,128)} %rest_0_.1, s32[3,256]{1,0:T(4,128)} %rest_1_.1), custom_call_target="tpu_custom_call" | custom-call | tf_op jit(solution)/shard_map/cut/pallas_call | solution.py:97
  16.2 0.0 collective-permute-done.4
  16.2 0.2 combine.4.refs_3_
  16.4 1.4 %collective-permute-done = bf16[36,2,2,128]{3,2,1,0:T(2,128)(2,1)S(1)} collective-permute-done((bf16[36,2,2,128]{3,2,1,0:T(2,128)(2,1)S(1)}, bf16[36,2,2,128]{3,2,1,0:T(2,128)(2,1)S(1)}, u32[]{:S(2)}, u32[]{:S(2)}) %collective-permute-start) | collective-permute-done | bytes 36896 | tf_op jit(solution)/shard_map/ppermute | solution.py:30
  17.9 0.0 collective-permute-done.1
  17.9 0.0 collective-permute-done.3.refs_2_
  17.9 0.1 combine.5.refs_0_
  18.0 1.6 %collective-permute-start.6 = (bf16[256,256]{1,0:T(8,128)(2,1)S(1)}, bf16[256,256]{1,0:T(8,128)(2,1)S(1)}, u32[]{:S(2)}, u32[]{:S(2)}) collective-permute-start(bf16[256,256]{1,0:T(8,128)(2,1)S(1)} %combine.5.refs_0_), channel_id=1, source_target_pairs={{0,16},{4,20},{8,24},{12,28},{16,0},{20,4},{24,8},{28,12},{1,17},{... | collective-permute-start | bytes 393224 | tf_op jit(solution)/shard_map/ppermute | solution.py:30
  19.6 1.5 %collective-permute-start.5 = (bf16[256,256]{1,0:T(8,128)(2,1)S(1)}, bf16[256,256]{1,0:T(8,128)(2,1)S(1)}, u32[]{:S(2)}, u32[]{:S(2)}) collective-permute-start(bf16[256,256]{1,0:T(8,128)(2,1)S(1)} %combine.5.refs_0_), channel_id=1, source_target_pairs={{0,8},{4,12},{8,0},{12,4},{16,24},{20,28},{24,16},{28,20},{1,9},{5... | collective-permute-start | bytes 393224 | tf_op jit(solution)/shard_map/ppermute | solution.py:30
  21.1 0.5 %collective-permute-start.8 = (bf16[256,256]{1,0:T(8,128)(2,1)S(1)}, bf16[256,256]{1,0:T(8,128)(2,1)S(1)}, u32[]{:S(2)}, u32[]{:S(2)}) collective-permute-start(bf16[256,256]{1,0:T(8,128)(2,1)S(1)} %combine.5.refs_0_), channel_id=1, source_target_pairs={{0,24},{4,28},{8,16},{12,20},{16,8},{20,12},{24,0},{28,4},{1,25},{... | collective-permute-start | bytes 393224 | tf_op jit(solution)/shard_map/ppermute | solution.py:30
  21.6 0.0 collective-permute-start.9
  21.6 1.5 %collective-permute-done.6.refs_2_ = bf16[256,256]{1,0:T(8,128)(2,1)S(1)} collective-permute-done((bf16[256,256]{1,0:T(8,128)(2,1)S(1)}, bf16[256,256]{1,0:T(8,128)(2,1)S(1)}, u32[]{:S(2)}, u32[]{:S(2)}) %collective-permute-start.6) | collective-permute-done | bytes 131104 | tf_op jit(solution)/shard_map/ppermute | solution.py:30
  23.1 0.0 collective-permute-start.7
  23.1 1.5 %collective-permute-done.5.refs_0_ = bf16[256,256]{1,0:T(8,128)(2,1)S(1)} collective-permute-done((bf16[256,256]{1,0:T(8,128)(2,1)S(1)}, bf16[256,256]{1,0:T(8,128)(2,1)S(1)}, u32[]{:S(2)}, u32[]{:S(2)}) %collective-permute-start.5) | collective-permute-done | bytes 131104 | tf_op jit(solution)/shard_map/ppermute | solution.py:30
  24.6 2.4 %collective-permute-done.8.refs_2_ = bf16[256,256]{1,0:T(8,128)(2,1)S(1)} collective-permute-done((bf16[256,256]{1,0:T(8,128)(2,1)S(1)}, bf16[256,256]{1,0:T(8,128)(2,1)S(1)}, u32[]{:S(2)}, u32[]{:S(2)}) %collective-permute-start.8) | collective-permute-done | bytes 131104 | tf_op jit(solution)/shard_map/ppermute | solution.py:30
  27.0 0.0 collective-permute-start.11
  27.0 0.9 %table.1.table_ref = bf16[8,256,512]{2,1,0:T(8,128)(2,1)S(1)} custom-call(s32[3,1024]{1,0:T(4,128)S(1)} %get-tuple-element.15.rp_ref, s32[3,256]{1,0:T(4,128)S(1)} %get-tuple-element.16.q_ref), custom_call_target="tpu_custom_call" | custom-call | flops 20971520 | bytes 2097152 | tf_op jit(solution)/shard_map/table/pallas_call | solution.py:243
  27.9 0.4 %partial.2.refs_3_ = f32[256,512]{1,0:T(8,128)S(1)} custom-call(bf16[8,256,512]{2,1,0:T(8,128)(2,1)S(1)} %table.1.table_ref, bf16[256,256]{1,0:T(8,128)(2,1)S(1)} %combine.5.refs_0_, bf16[256,256]{1,0:T(8,128)(2,1)S(1)} %collective-permute-done.9.refs_1_, bf16[256,256]{1,0:T(8,128)(2,1)S(1)} %collective-permute-done.6.refs_2_), custom_call_target="tpu_custom_call" | custom-call | flops 201326592 | bytes 524288 | tf_op jit(solution)/shard_map/partial/pallas_call | solution.py:279
  28.3 0.0 copy-start
  28.3 0.4 %partial.3.sum_ref = f32[256,512]{1,0:T(8,128)S(1)} custom-call(bf16[8,256,512]{2,1,0:T(8,128)(2,1)S(1)} %table.1.table_ref, bf16[256,256]{1,0:T(8,128)(2,1)S(1)} %collective-permute-done.5.refs_0_, bf16[256,256]{1,0:T(8,128)(2,1)S(1)} %collective-permute-done.7.refs_1_, bf16[256,256]{1,0:T(8,128)(2,1)S(1)} %collective-permute-done.8.refs_2_, ...), custom_call_target="tpu_custom_call" | custom-call | flops 201326592 | bytes 524288 | tf_op jit(solution)/shard_map/partial/pallas_call | solution.py:279
  28.7 0.0 collective-permute-done.10.refs_0_
  28.7 0.0 collective-permute-done.11.refs_1_
  28.7 0.3 copy-done
  29.0 1.1 %finish.1 = f32[2,2,128,256]{3,2,1,0:T(8,128)} custom-call(bf16[8,256,512]{2,1,0:T(8,128)(2,1)S(1)} %table.1.table_ref, f32[16,256]{1,0:T(8,128)S(1)} %copy-done, f32[256,512]{1,0:T(8,128)S(1)} %partial.3.sum_ref, bf16[256,256]{1,0:T(8,128)(2,1)S(1)} %collective-permute-done.10.refs_0_, bf16[256,256]{1,0:T(8,128)(2,1)S(1)} %collective-permute-done.11.refs_1_), custom_call_target="tpu_custom_call" | custom-call | tf_op jit(solution)/shard_map/finish/pallas_call | solution.py:324
  (3 shorter events, 0.0 us)
Async XLA Ops:
  1.1 6.7 %collective-permute-start.2 = (bf16[100,2,2,128]{3,2,1,0:T(2,128)(2,1)S(1)}, bf16[100,2,2,128]{3,2,1,0:T(2,128)(2,1)S(1)}, u32[]{:S(2)}, u32[]{:S(2)}) collective-permute-start(bf16[100,2,2,128]{3,2,1,0:T(2,128)(2,1)S(1)} %get-tuple-element.22), channel_id=1, source_target_pairs={{0,1},{1,0},{2,3},{3,2},{4,5},{5,4},{6,7},{7,6},{8,9},{9,8},{10,11... | collective-permute-start | bytes 307208 | tf_op jit(solution)/shard_map/ppermute | solution.py:30
  4.2 12.0 %collective-permute-start.4 = (bf16[132,2,2,128]{3,2,1,0:T(2,128)(2,1)S(1)}, bf16[132,2,2,128]{3,2,1,0:T(2,128)(2,1)S(1)}, u32[]{:S(2)}, u32[]{:S(2)}) collective-permute-start(bf16[132,2,2,128]{3,2,1,0:T(2,128)(2,1)S(1)} %get-tuple-element.24), channel_id=1, source_target_pairs={{0,1},{1,0},{2,3},{3,2},{4,5},{5,4},{6,7},{7,6},{8,9},{9,8},{10,11... | collective-permute-start | bytes 405512 | tf_op jit(solution)/shard_map/ppermute | solution.py:30
  8.1 9.8 %collective-permute-start.3 = (s16[208,256]{1,0:T(8,128)(2,1)S(1)}, s16[208,256]{1,0:T(8,128)(2,1)S(1)}, u32[]{:S(2)}, u32[]{:S(2)}) collective-permute-start(s16[208,256]{1,0:T(8,128)(2,1)S(1)} %combine.3), channel_id=1, source_target_pairs={{0,2},{1,3},{2,0},{3,1},{4,6},{5,7},{6,4},{7,5},{8,10},{9,11},{10,... | collective-permute-start | bytes 319496 | tf_op jit(solution)/shard_map/ppermute | solution.py:30
  11.1 6.8 %collective-permute-start = (bf16[36,2,2,128]{3,2,1,0:T(2,128)(2,1)S(1)}, bf16[36,2,2,128]{3,2,1,0:T(2,128)(2,1)S(1)}, u32[]{:S(2)}, u32[]{:S(2)}) collective-permute-start(bf16[36,2,2,128]{3,2,1,0:T(2,128)(2,1)S(1)} %get-tuple-element.19), channel_id=1, source_target_pairs={{0,2},{1,3},{2,0},{3,1},{4,6},{5,7},{6,4},{7,5},{8,10},{9,11},{10,... | collective-permute-start | bytes 110600 | tf_op jit(solution)/shard_map/ppermute | solution.py:30
  11.2 6.7 %collective-permute-start.1 = (bf16[36,2,2,128]{3,2,1,0:T(2,128)(2,1)S(1)}, bf16[36,2,2,128]{3,2,1,0:T(2,128)(2,1)S(1)}, u32[]{:S(2)}, u32[]{:S(2)}) collective-permute-start(bf16[36,2,2,128]{3,2,1,0:T(2,128)(2,1)S(1)} %get-tuple-element.20), channel_id=1, source_target_pairs={{0,3},{1,2},{2,1},{3,0},{4,7},{5,6},{6,5},{7,4},{8,11},{9,10},{10,... | collective-permute-start | bytes 110600 | tf_op jit(solution)/shard_map/ppermute | solution.py:30
  18.0 5.1 %collective-permute-start.6 = (bf16[256,256]{1,0:T(8,128)(2,1)S(1)}, bf16[256,256]{1,0:T(8,128)(2,1)S(1)}, u32[]{:S(2)}, u32[]{:S(2)}) collective-permute-start(bf16[256,256]{1,0:T(8,128)(2,1)S(1)} %combine.5.refs_0_), channel_id=1, source_target_pairs={{0,16},{4,20},{8,24},{12,28},{16,0},{20,4},{24,8},{28,12},{1,17},{... | collective-permute-start | bytes 393224 | tf_op jit(solution)/shard_map/ppermute | solution.py:30
  19.6 5.0 %collective-permute-start.5 = (bf16[256,256]{1,0:T(8,128)(2,1)S(1)}, bf16[256,256]{1,0:T(8,128)(2,1)S(1)}, u32[]{:S(2)}, u32[]{:S(2)}) collective-permute-start(bf16[256,256]{1,0:T(8,128)(2,1)S(1)} %combine.5.refs_0_), channel_id=1, source_target_pairs={{0,8},{4,12},{8,0},{12,4},{16,24},{20,28},{24,16},{28,20},{1,9},{5... | collective-permute-start | bytes 393224 | tf_op jit(solution)/shard_map/ppermute | solution.py:30
  21.1 5.9 %collective-permute-start.8 = (bf16[256,256]{1,0:T(8,128)(2,1)S(1)}, bf16[256,256]{1,0:T(8,128)(2,1)S(1)}, u32[]{:S(2)}, u32[]{:S(2)}) collective-permute-start(bf16[256,256]{1,0:T(8,128)(2,1)S(1)} %combine.5.refs_0_), channel_id=1, source_target_pairs={{0,24},{4,28},{8,16},{12,20},{16,8},{20,12},{24,0},{28,4},{1,25},{... | collective-permute-start | bytes 393224 | tf_op jit(solution)/shard_map/ppermute | solution.py:30
  21.6 6.3 %collective-permute-start.9 = (bf16[256,256]{1,0:T(8,128)(2,1)S(1)}, bf16[256,256]{1,0:T(8,128)(2,1)S(1)}, u32[]{:S(2)}, u32[]{:S(2)}) collective-permute-start(bf16[256,256]{1,0:T(8,128)(2,1)S(1)} %combine.5.refs_0_), channel_id=1, source_target_pairs={{0,4},{4,0},{8,12},{12,8},{16,20},{20,16},{24,28},{28,24},{1,5},{5... | collective-permute-start | bytes 393224 | tf_op jit(solution)/shard_map/ppermute | solution.py:30
  23.1 5.2 %collective-permute-start.7 = (bf16[256,256]{1,0:T(8,128)(2,1)S(1)}, bf16[256,256]{1,0:T(8,128)(2,1)S(1)}, u32[]{:S(2)}, u32[]{:S(2)}) collective-permute-start(bf16[256,256]{1,0:T(8,128)(2,1)S(1)} %collective-permute-done.6.refs_2_), channel_id=1, source_target_pairs={{0,4},{4,0},{8,12},{12,8},{16,20},{20,16},{24,28},{28,24},{1,5},{5... | collective-permute-start | bytes 393224 | tf_op jit(solution)/shard_map/ppermute | solution.py:30
  24.6 4.2 %collective-permute-start.10 = (bf16[256,256]{1,0:T(8,128)(2,1)S(1)}, bf16[256,256]{1,0:T(8,128)(2,1)S(1)}, u32[]{:S(2)}, u32[]{:S(2)}) collective-permute-start(bf16[256,256]{1,0:T(8,128)(2,1)S(1)} %collective-permute-done.5.refs_0_), channel_id=1, source_target_pairs={{0,4},{4,0},{8,12},{12,8},{16,20},{20,16},{24,28},{28,24},{1,5},{5... | collective-permute-start | bytes 393224 | tf_op jit(solution)/shard_map/ppermute | solution.py:30
  27.0 1.8 %collective-permute-start.11 = (bf16[256,256]{1,0:T(8,128)(2,1)S(1)}, bf16[256,256]{1,0:T(8,128)(2,1)S(1)}, u32[]{:S(2)}, u32[]{:S(2)}) collective-permute-start(bf16[256,256]{1,0:T(8,128)(2,1)S(1)} %collective-permute-done.8.refs_2_), channel_id=1, source_target_pairs={{0,4},{4,0},{8,12},{12,8},{16,20},{20,16},{24,28},{28,24},{1,5},{5... | collective-permute-start | bytes 393224 | tf_op jit(solution)/shard_map/ppermute | solution.py:30
  28.3 0.7 %copy-start = (f32[16,256]{1,0:T(8,128)S(1)}, f32[16,256]{1,0:T(8,128)}, u32[]{:S(2)}) copy-start(f32[16,256]{1,0:T(8,128)} %energy_ref.1) | copy-start | bytes 49156

commit v5 on v4

--- a/solution.py
+++ b/solution.py
@@ -13,11 +13,11 @@
 MESHQ = 32
 MESHK = 32
 LANES = 128
-TAIL = 4
-NEAR = (4, 6, 2)
+TAIL = 2
+NEAR = (6, 4, 2)
 LAST = 96
 ORDER = ("pair", "two", "three", "one", "sum")
-EARLY = 1
+EARLY = 0
 CODED = 1
 BITS = 14.0
 

time: 30.3 us -> 29.4 us (0.970)
  waiting for transfers between devices: 10.4 us -> 9.44 us
    ppermute x12, waiting for transfers between devices: 10.4 us -> 9.44 us  [swap(): return lax.ppermute(value, axis, xor_pairs(count, step))]
where the time goes in v5:
time: 29.4 us; the launch traced here: 29.1 us
  starting transfers between devices  14 us (48%)
  waiting for transfers between devices  9.44 us (32%)
  Pallas kernels  5.34 us (18%)
    ppermute x12, starting transfers between devices, swap(): return lax.ppermute(value, axis, xor_pairs(count, step))  14 us
    ppermute x12, waiting for transfers between devices, swap(): return lax.ppermute(value, axis, xor_pairs(count, step))  9.44 us
    pallas_call x2, Pallas kernels, cut(): pl.pallas_call(functools.partial(cut_kernel, parts, rings, len(extra), en...  2.1 us
    pallas_call x1, Pallas kernels, finish(): pl.pallas_call(functools.partial(finish_kernel, pieces, waves, entries),...  1.06 us
    pallas_call x1, Pallas kernels, table(): pl.pallas_call(functools.partial(table_kernel, slab), out_shape=jax.Shape...  0.91 us
    pallas_call x2, Pallas kernels, partial(): pl.pallas_call(functools.partial(partial_kernel, pieces, bool(more)), out...  0.78 us
  transfers between devices with their start and end apart: 12, of which 5 were waited for; matrix products, arithmetic and copies ran while one was open for 0% of the time, Pallas kernels for 10%

profile of v5, /device:TPU:0, one launch (start us, length us, event | category | flops | bytes accessed | tf_op | source)
XLA Modules:
  0.0 29.1 jit_solution(852408837458559071)
XLA Ops:
  0.0 1.1 %cut.3 = (bf16[98,2,2,128]{3,2,1,0:T(2,128)(2,1)S(1)}, bf16[34,2,2,128]{3,2,1,0:T(2,128)(2,1)S(1)}, bf16[34,2,2,128]{3,2,1,0:T(2,128)(2,1)S(1)}, bf16[130,2,2,12...) custom-call(bf16[128,2,2,512]{3,2,1,0:T(2,128)(2,1)} %x_ref.3, ...), custom_call_target="tpu_custom_call" | custom-call | tf_op jit(solution)/shard_map/cut/pallas_call | solution.py:97
  1.1 3.1 %collective-permute-start.3 = (bf16[98,2,2,128]{3,2,1,0:T(2,128)(2,1)S(1)}, bf16[98,2,2,128]{3,2,1,0:T(2,128)(2,1)S(1)}, u32[]{:S(2)}, u32[]{:S(2)}) collective-permute-start(bf16[98,2,2,128]{3,2,1,0:T(2,128)(2,1)S(1)} %get-tuple-element.24), channel_id=1, source_target_pairs={{0,1},{1,0},{2,3},{3,2},{4,5},{5,4},{6,7},{7,6},{8,9},{9,8},{10,11... | collective-permute-start | bytes 301064 | tf_op jit(solution)/shard_map/ppermute | solution.py:30
  4.2 0.1 collective-permute-start
  4.3 3.4 %collective-permute-done.3 = bf16[98,2,2,128]{3,2,1,0:T(2,128)(2,1)S(1)} collective-permute-done((bf16[98,2,2,128]{3,2,1,0:T(2,128)(2,1)S(1)}, bf16[98,2,2,128]{3,2,1,0:T(2,128)(2,1)S(1)}, u32[]{:S(2)}, u32[]{:S(2)}) %collective-permute-start.3) | collective-permute-done | bytes 100384 | tf_op jit(solution)/shard_map/ppermute | solution.py:30
  7.8 0.2 combine.2
  8.0 3.1 %collective-permute-start.4 = (s16[208,256]{1,0:T(8,128)(2,1)S(1)}, s16[208,256]{1,0:T(8,128)(2,1)S(1)}, u32[]{:S(2)}, u32[]{:S(2)}) collective-permute-start(s16[208,256]{1,0:T(8,128)(2,1)S(1)} %combine.2), channel_id=1, source_target_pairs={{0,2},{1,3},{2,0},{3,1},{4,6},{5,7},{6,4},{7,5},{8,10},{9,11},{10,... | collective-permute-start | bytes 319496 | tf_op jit(solution)/shard_map/ppermute | solution.py:30
  11.1 0.1 collective-permute-start.1
  11.2 4.0 %collective-permute-start.2 = (bf16[34,2,2,128]{3,2,1,0:T(2,128)(2,1)S(1)}, bf16[34,2,2,128]{3,2,1,0:T(2,128)(2,1)S(1)}, u32[]{:S(2)}, u32[]{:S(2)}) collective-permute-start(bf16[34,2,2,128]{3,2,1,0:T(2,128)(2,1)S(1)} %get-tuple-element.22), channel_id=1, source_target_pairs={{0,3},{1,2},{2,1},{3,0},{4,7},{5,6},{6,5},{7,4},{8,11},{9,10},{10,... | collective-permute-start | bytes 104456 | tf_op jit(solution)/shard_map/ppermute | solution.py:30
  15.2 1.0 %cut.2 = (bf16[130,2,2,128]{3,2,1,0:T(2,128)(2,1)S(1)}, s32[3,1024]{1,0:T(4,128)S(1)}, s32[3,256]{1,0:T(4,128)S(1)}) custom-call(bf16[128,2,2,512]{3,2,1,0:T(2,128)(2,1)} %x_ref.3, s32[2,3]{1,0:T(2,128)} %bitcast.15, s32[2,3]{1,0:T(2,128)} %bitcast.17, s32[3,1024]{1,0:T(4,128)} %rest_0_.1, s32[3,256]{1,0:T(4,128)} %rest_1_.1), custom_call_target="tpu_custom_call" | custom-call | tf_op jit(solution)/shard_map/cut/pallas_call | solution.py:97
  16.2 1.5 %collective-permute-done.1 = bf16[34,2,2,128]{3,2,1,0:T(2,128)(2,1)S(1)} collective-permute-done((bf16[34,2,2,128]{3,2,1,0:T(2,128)(2,1)S(1)}, bf16[34,2,2,128]{3,2,1,0:T(2,128)(2,1)S(1)}, u32[]{:S(2)}, u32[]{:S(2)}) %collective-permute-start.1) | collective-permute-done | bytes 34848 | tf_op jit(solution)/shard_map/ppermute | solution.py:30
  17.7 0.0 collective-permute-done.2
  17.7 0.0 collective-permute-done
  17.7 0.0 collective-permute-done.4.refs_4_
  17.7 0.3 combine.3.refs_0_
  18.0 2.5 %collective-permute-start.6 = (bf16[256,256]{1,0:T(8,128)(2,1)S(1)}, bf16[256,256]{1,0:T(8,128)(2,1)S(1)}, u32[]{:S(2)}, u32[]{:S(2)}) collective-permute-start(bf16[256,256]{1,0:T(8,128)(2,1)S(1)} %combine.3.refs_0_), channel_id=1, source_target_pairs={{0,24},{4,28},{8,16},{12,20},{16,8},{20,12},{24,0},{28,4},{1,25},{... | collective-permute-start | bytes 393224 | tf_op jit(solution)/shard_map/ppermute | solution.py:30
  20.5 0.5 %collective-permute-start.5 = (bf16[256,256]{1,0:T(8,128)(2,1)S(1)}, bf16[256,256]{1,0:T(8,128)(2,1)S(1)}, u32[]{:S(2)}, u32[]{:S(2)}) collective-permute-start(bf16[256,256]{1,0:T(8,128)(2,1)S(1)} %combine.3.refs_0_), channel_id=1, source_target_pairs={{0,8},{4,12},{8,0},{12,4},{16,24},{20,28},{24,16},{28,20},{1,9},{5... | collective-permute-start | bytes 393224 | tf_op jit(solution)/shard_map/ppermute | solution.py:30
  21.1 0.5 %collective-permute-start.8 = (bf16[256,256]{1,0:T(8,128)(2,1)S(1)}, bf16[256,256]{1,0:T(8,128)(2,1)S(1)}, u32[]{:S(2)}, u32[]{:S(2)}) collective-permute-start(bf16[256,256]{1,0:T(8,128)(2,1)S(1)} %combine.3.refs_0_), channel_id=1, source_target_pairs={{0,16},{4,20},{8,24},{12,28},{16,0},{20,4},{24,8},{28,12},{1,17},{... | collective-permute-start | bytes 393224 | tf_op jit(solution)/shard_map/ppermute | solution.py:30
  21.6 0.0 collective-permute-start.9
  21.6 2.4 %collective-permute-done.6.refs_2_ = bf16[256,256]{1,0:T(8,128)(2,1)S(1)} collective-permute-done((bf16[256,256]{1,0:T(8,128)(2,1)S(1)}, bf16[256,256]{1,0:T(8,128)(2,1)S(1)}, u32[]{:S(2)}, u32[]{:S(2)}) %collective-permute-start.6) | collective-permute-done | bytes 131104 | tf_op jit(solution)/shard_map/ppermute | solution.py:30
  23.9 0.0 collective-permute-start.7
  23.9 1.5 %collective-permute-done.5.refs_0_ = bf16[256,256]{1,0:T(8,128)(2,1)S(1)} collective-permute-done((bf16[256,256]{1,0:T(8,128)(2,1)S(1)}, bf16[256,256]{1,0:T(8,128)(2,1)S(1)}, u32[]{:S(2)}, u32[]{:S(2)}) %collective-permute-start.5) | collective-permute-done | bytes 131104 | tf_op jit(solution)/shard_map/ppermute | solution.py:30
  25.5 0.0 collective-permute-start.10
  25.5 0.5 %collective-permute-done.8.refs_2_ = bf16[256,256]{1,0:T(8,128)(2,1)S(1)} collective-permute-done((bf16[256,256]{1,0:T(8,128)(2,1)S(1)}, bf16[256,256]{1,0:T(8,128)(2,1)S(1)}, u32[]{:S(2)}, u32[]{:S(2)}) %collective-permute-start.8) | collective-permute-done | bytes 131104 | tf_op jit(solution)/shard_map/ppermute | solution.py:30
  26.0 0.9 %table.1.table_ref = bf16[8,256,512]{2,1,0:T(8,128)(2,1)S(1)} custom-call(s32[3,1024]{1,0:T(4,128)S(1)} %get-tuple-element.15.rp_ref, s32[3,256]{1,0:T(4,128)S(1)} %get-tuple-element.16.q_ref), custom_call_target="tpu_custom_call" | custom-call | flops 20971520 | bytes 2097152 | tf_op jit(solution)/shard_map/table/pallas_call | solution.py:243
  26.9 0.0 collective-permute-done.9.refs_1_
  26.9 0.4 %partial.2.refs_3_ = f32[256,512]{1,0:T(8,128)S(1)} custom-call(bf16[8,256,512]{2,1,0:T(8,128)(2,1)S(1)} %table.1.table_ref, bf16[256,256]{1,0:T(8,128)(2,1)S(1)} %combine.3.refs_0_, bf16[256,256]{1,0:T(8,128)(2,1)S(1)} %collective-permute-done.9.refs_1_, bf16[256,256]{1,0:T(8,128)(2,1)S(1)} %collective-permute-done.6.refs_2_), custom_call_target="tpu_custom_call" | custom-call | flops 201326592 | bytes 524288 | tf_op jit(solution)/shard_map/partial/pallas_call | solution.py:279
  27.3 0.0 copy-start
  27.4 0.0 collective-permute-done.7.refs_1_
  27.4 0.4 %partial.3.sum_ref = f32[256,512]{1,0:T(8,128)S(1)} custom-call(bf16[8,256,512]{2,1,0:T(8,128)(2,1)S(1)} %table.1.table_ref, bf16[256,256]{1,0:T(8,128)(2,1)S(1)} %collective-permute-done.5.refs_0_, bf16[256,256]{1,0:T(8,128)(2,1)S(1)} %collective-permute-done.7.refs_1_, bf16[256,256]{1,0:T(8,128)(2,1)S(1)} %collective-permute-done.8.refs_2_, ...), custom_call_target="tpu_custom_call" | custom-call | flops 201326592 | bytes 524288 | tf_op jit(solution)/shard_map/partial/pallas_call | solution.py:279
  27.8 0.0 collective-permute-done.11.refs_1_
  27.8 0.3 copy-done
  28.1 1.1 %finish.1 = f32[2,2,128,256]{3,2,1,0:T(8,128)} custom-call(bf16[8,256,512]{2,1,0:T(8,128)(2,1)S(1)} %table.1.table_ref, f32[16,256]{1,0:T(8,128)S(1)} %copy-done, f32[256,512]{1,0:T(8,128)S(1)} %partial.3.sum_ref, bf16[256,256]{1,0:T(8,128)(2,1)S(1)} %collective-permute-done.10.refs_0_, bf16[256,256]{1,0:T(8,128)(2,1)S(1)} %collective-permute-done.11.refs_1_), custom_call_target="tpu_custom_call" | custom-call | tf_op jit(solution)/shard_map/finish/pallas_call | solution.py:324
  (2 shorter events, 0.0 us)
Async XLA Ops:
  1.1 6.6 %collective-permute-start.3 = (bf16[98,2,2,128]{3,2,1,0:T(2,128)(2,1)S(1)}, bf16[98,2,2,128]{3,2,1,0:T(2,128)(2,1)S(1)}, u32[]{:S(2)}, u32[]{:S(2)}) collective-permute-start(bf16[98,2,2,128]{3,2,1,0:T(2,128)(2,1)S(1)} %get-tuple-element.24), channel_id=1, source_target_pairs={{0,1},{1,0},{2,3},{3,2},{4,5},{5,4},{6,7},{7,6},{8,9},{9,8},{10,11... | collective-permute-start | bytes 301064 | tf_op jit(solution)/shard_map/ppermute | solution.py:30
  4.2 13.5 %collective-permute-start = (bf16[130,2,2,128]{3,2,1,0:T(2,128)(2,1)S(1)}, bf16[130,2,2,128]{3,2,1,0:T(2,128)(2,1)S(1)}, u32[]{:S(2)}, u32[]{:S(2)}) collective-permute-start(bf16[130,2,2,128]{3,2,1,0:T(2,128)(2,1)S(1)} %get-tuple-element.20), channel_id=1, source_target_pairs={{0,1},{1,0},{2,3},{3,2},{4,5},{5,4},{6,7},{7,6},{8,9},{9,8},{10,11... | collective-permute-start | bytes 399368 | tf_op jit(solution)/shard_map/ppermute | solution.py:30
  8.0 9.7 %collective-permute-start.4 = (s16[208,256]{1,0:T(8,128)(2,1)S(1)}, s16[208,256]{1,0:T(8,128)(2,1)S(1)}, u32[]{:S(2)}, u32[]{:S(2)}) collective-permute-start(s16[208,256]{1,0:T(8,128)(2,1)S(1)} %combine.2), channel_id=1, source_target_pairs={{0,2},{1,3},{2,0},{3,1},{4,6},{5,7},{6,4},{7,5},{8,10},{9,11},{10,... | collective-permute-start | bytes 319496 | tf_op jit(solution)/shard_map/ppermute | solution.py:30
  11.1 6.6 %collective-permute-start.1 = (bf16[34,2,2,128]{3,2,1,0:T(2,128)(2,1)S(1)}, bf16[34,2,2,128]{3,2,1,0:T(2,128)(2,1)S(1)}, u32[]{:S(2)}, u32[]{:S(2)}) collective-permute-start(bf16[34,2,2,128]{3,2,1,0:T(2,128)(2,1)S(1)} %get-tuple-element.21), channel_id=1, source_target_pairs={{0,2},{1,3},{2,0},{3,1},{4,6},{5,7},{6,4},{7,5},{8,10},{9,11},{10,... | collective-permute-start | bytes 104456 | tf_op jit(solution)/shard_map/ppermute | solution.py:30
  11.2 6.5 %collective-permute-start.2 = (bf16[34,2,2,128]{3,2,1,0:T(2,128)(2,1)S(1)}, bf16[34,2,2,128]{3,2,1,0:T(2,128)(2,1)S(1)}, u32[]{:S(2)}, u32[]{:S(2)}) collective-permute-start(bf16[34,2,2,128]{3,2,1,0:T(2,128)(2,1)S(1)} %get-tuple-element.22), channel_id=1, source_target_pairs={{0,3},{1,2},{2,1},{3,0},{4,7},{5,6},{6,5},{7,4},{8,11},{9,10},{10,... | collective-permute-start | bytes 104456 | tf_op jit(solution)/shard_map/ppermute | solution.py:30
  18.0 5.9 %collective-permute-start.6 = (bf16[256,256]{1,0:T(8,128)(2,1)S(1)}, bf16[256,256]{1,0:T(8,128)(2,1)S(1)}, u32[]{:S(2)}, u32[]{:S(2)}) collective-permute-start(bf16[256,256]{1,0:T(8,128)(2,1)S(1)} %combine.3.refs_0_), channel_id=1, source_target_pairs={{0,24},{4,28},{8,16},{12,20},{16,8},{20,12},{24,0},{28,4},{1,25},{... | collective-permute-start | bytes 393224 | tf_op jit(solution)/shard_map/ppermute | solution.py:30
  20.5 5.0 %collective-permute-start.5 = (bf16[256,256]{1,0:T(8,128)(2,1)S(1)}, bf16[256,256]{1,0:T(8,128)(2,1)S(1)}, u32[]{:S(2)}, u32[]{:S(2)}) collective-permute-start(bf16[256,256]{1,0:T(8,128)(2,1)S(1)} %combine.3.refs_0_), channel_id=1, source_target_pairs={{0,8},{4,12},{8,0},{12,4},{16,24},{20,28},{24,16},{28,20},{1,9},{5... | collective-permute-start | bytes 393224 | tf_op jit(solution)/shard_map/ppermute | solution.py:30
  21.1 5.0 %collective-permute-start.8 = (bf16[256,256]{1,0:T(8,128)(2,1)S(1)}, bf16[256,256]{1,0:T(8,128)(2,1)S(1)}, u32[]{:S(2)}, u32[]{:S(2)}) collective-permute-start(bf16[256,256]{1,0:T(8,128)(2,1)S(1)} %combine.3.refs_0_), channel_id=1, source_target_pairs={{0,16},{4,20},{8,24},{12,28},{16,0},{20,4},{24,8},{28,12},{1,17},{... | collective-permute-start | bytes 393224 | tf_op jit(solution)/shard_map/ppermute | solution.py:30
  21.6 5.4 %collective-permute-start.9 = (bf16[256,256]{1,0:T(8,128)(2,1)S(1)}, bf16[256,256]{1,0:T(8,128)(2,1)S(1)}, u32[]{:S(2)}, u32[]{:S(2)}) collective-permute-start(bf16[256,256]{1,0:T(8,128)(2,1)S(1)} %combine.3.refs_0_), channel_id=1, source_target_pairs={{0,4},{4,0},{8,12},{12,8},{16,20},{20,16},{24,28},{28,24},{1,5},{5... | collective-permute-start | bytes 393224 | tf_op jit(solution)/shard_map/ppermute | solution.py:30
  23.9 3.4 %collective-permute-start.7 = (bf16[256,256]{1,0:T(8,128)(2,1)S(1)}, bf16[256,256]{1,0:T(8,128)(2,1)S(1)}, u32[]{:S(2)}, u32[]{:S(2)}) collective-permute-start(bf16[256,256]{1,0:T(8,128)(2,1)S(1)} %collective-permute-done.6.refs_2_), channel_id=1, source_target_pairs={{0,4},{4,0},{8,12},{12,8},{16,20},{20,16},{24,28},{28,24},{1,5},{5... | collective-permute-start | bytes 393224 | tf_op jit(solution)/shard_map/ppermute | solution.py:30
  25.5 2.3 %collective-permute-start.10 = (bf16[256,256]{1,0:T(8,128)(2,1)S(1)}, bf16[256,256]{1,0:T(8,128)(2,1)S(1)}, u32[]{:S(2)}, u32[]{:S(2)}) collective-permute-start(bf16[256,256]{1,0:T(8,128)(2,1)S(1)} %collective-permute-done.5.refs_0_), channel_id=1, source_target_pairs={{0,4},{4,0},{8,12},{12,8},{16,20},{20,16},{24,28},{28,24},{1,5},{5... | collective-permute-start | bytes 393224 | tf_op jit(solution)/shard_map/ppermute | solution.py:30
  26.0 1.8 %collective-permute-start.11 = (bf16[256,256]{1,0:T(8,128)(2,1)S(1)}, bf16[256,256]{1,0:T(8,128)(2,1)S(1)}, u32[]{:S(2)}, u32[]{:S(2)}) collective-permute-start(bf16[256,256]{1,0:T(8,128)(2,1)S(1)} %collective-permute-done.8.refs_2_), channel_id=1, source_target_pairs={{0,4},{4,0},{8,12},{12,8},{16,20},{20,16},{24,28},{28,24},{1,5},{5... | collective-permute-start | bytes 393224 | tf_op jit(solution)/shard_map/ppermute | solution.py:30
  27.3 0.7 %copy-start = (f32[16,256]{1,0:T(8,128)S(1)}, f32[16,256]{1,0:T(8,128)}, u32[]{:S(2)}) copy-start(f32[16,256]{1,0:T(8,128)} %energy_ref.1) | copy-start | bytes 49156
